TPU v7x, 512 devices: a whole 4x8x8 slice. The times are simulated.
512 devices in a mesh: sub: 64 (over y, z), crow: 4 (over x_lo, core), ccol: 2 (over x_hi).
Axes of the slice: x: 4 (x_hi: 2, x_lo: 2; x = x_hi * 2 + x_lo), y: 8, z: 8, core: 2. Of those that a mesh axis runs over, the one named last changes fastest.
Arguments:
- loads: bfloat16 [128, 1024, 128], P('sub'), may hold values from -6 to 6
- stiffness: bfloat16 [128, 1024, 1024], P('sub', ('crow', 'ccol'))
- local_inverse: bfloat16 [128, 1024, 1024], P('sub', ('crow', 'ccol'))
- coarse_basis: bfloat16 [128, 1024, 48], P('sub', ('crow', 'ccol')), may hold values from -0.1875 to 0.1875
- coarse_inverse: bfloat16 [6144, 6144], P('sub', ('crow', 'ccol'))
- coarse_index: int32 [128, 48], P('sub'), may hold values from 0 to 6143, as said below
- left_rows: int32 [128, 128], P('sub'), may hold values from 0 to 1023, as said below
- right_rows: int32 [128, 128], P('sub'), may hold values from 0 to 1023, as said below
Outputs:
- second_pass: float32 [128, 1024, 128], P('sub', ('crow', 'ccol'))
- final_residual: float32 [128, 1024, 128], P('sub', ('crow', 'ccol'))
Inputs may be any that keep to these rules, and one draw needn't show every extreme that they name: `coarse_index`: every value 0 to 6143 appears exactly once in the whole array. Of the 96 values in the rows of one index of sub, at most 24 lie in one block of 768 consecutive coarse rows starting at a multiple of 768, and that most is reached. In each subdomain the 128 entries of left_rows and the 128 entries of right_rows are 256 distinct rows. `right_rows`: see left_rows.
All inputs are finite; a program needn't handle non-finite values.
Results may differ from a plain program's by a relative error of at most 0.0067.
Values may be sent and summed in bfloat16 or wider, within the bound.
A program may use at most 64 MiB of HBM per device.

v0:
```python
import jax
import jax.numpy as jnp
from jax import lax
from jax.sharding import PartitionSpec as P


def padded(block, sides, width):
    for axis, dim in sides:
        count = lax.axis_size(axis)
        forward = [(i, i + 1) for i in range(count - 1)]
        forward.append((count - 1, 0))
        backward = [(target, source) for source, target in forward]
        low = lax.ppermute(
            lax.slice_in_dim(block, block.shape[dim] - width, None, axis=dim), axis, forward
        )
        high = lax.ppermute(lax.slice_in_dim(block, 0, width, axis=dim), axis, backward)
        block = jnp.concatenate([low, block, high], axis=dim)
    return block


def fold_product(matrix, gathered_piece):
    return jnp.einsum("sij,sjc->sic", matrix, gathered_piece, preferred_element_type=jnp.float32)


def apply_stiffness(iterate, stiffness, pick_left, pick_right):
    sub_count, row_count, case_count = iterate.shape
    rounded = iterate.astype(jnp.bfloat16)
    product = fold_product(stiffness, lax.all_gather(rounded, ("crow", "ccol"), axis=1, tiled=True))
    product_b = product.astype(jnp.bfloat16)
    left_part = jnp.einsum("sfi,sic->sfc", pick_left, product_b, preferred_element_type=jnp.float32)
    right_part = jnp.einsum(
        "sfi,sic->sfc", pick_right, product_b, preferred_element_type=jnp.float32
    )
    partial_faces = jnp.stack([left_part, right_part], axis=1)
    boundary = lax.psum(partial_faces.astype(jnp.bfloat16), ("crow", "ccol"))
    extended = padded(boundary, (("sub", 0),), 1)
    from_before = extended[:sub_count, 1]
    from_after = extended[2:, 0]
    added_left = jnp.einsum(
        "sfi,sfc->sic", pick_left, from_before, preferred_element_type=jnp.float32
    )
    added_right = jnp.einsum(
        "sfi,sfc->sic", pick_right, from_after, preferred_element_type=jnp.float32
    )
    return product_b.astype(jnp.float32) + added_left + added_right


def coarse_step(restricted, coarse_inverse, coarse_index):
    sub_count, mode_count, case_count = restricted.shape
    flat_rows = restricted.reshape(sub_count * mode_count, case_count)
    flat_index = coarse_index.reshape(-1)
    owned_rows, block_width = coarse_inverse.shape
    block_index = lax.axis_index(("crow", "ccol"))
    arrived, arrived_index = (
        lax.all_gather(flat_rows, "sub", axis=0, tiled=True),
        lax.all_gather(flat_index, "sub", axis=0, tiled=True),
    )
    shifted_place = arrived_index - block_index * block_width
    inside = (shifted_place >= 0) & (shifted_place < block_width)
    arrived_place = jnp.where(inside, shifted_place, block_width)
    ordered = (
        jnp.zeros((block_width + 1, case_count), jnp.bfloat16)
        .at[arrived_place]
        .set(arrived)[:block_width]
    )
    partial_coarse = jnp.dot(coarse_inverse, ordered, preferred_element_type=jnp.float32)
    coarse = lax.psum(partial_coarse, ("crow", "ccol")).astype(jnp.bfloat16)
    everything = lax.all_gather(coarse, "sub", axis=0, tiled=True)
    picked = everything[flat_index]
    return picked.reshape(sub_count, mode_count, case_count)


def precondition(local_part, residual_rows, coarse_basis, coarse_inverse, coarse_index):
    partial_modes = jnp.einsum(
        "sik,sic->skc", coarse_basis, residual_rows, preferred_element_type=jnp.float32
    )
    restricted = lax.psum(partial_modes, ("crow", "ccol")).astype(jnp.bfloat16)
    picked = coarse_step(restricted, coarse_inverse, coarse_index)
    return local_part + jnp.einsum(
        "sik,skc->sic", coarse_basis, picked, preferred_element_type=jnp.float32
    )


def body(
    loads,
    stiffness,
    local_inverse,
    coarse_basis,
    coarse_inverse,
    coarse_index,
    left_rows,
    right_rows,
):
    sub_count, row_count, iface_count = stiffness.shape
    group_index = lax.axis_index(("crow", "ccol"))
    first_row = group_index * row_count
    loads_rows = lax.dynamic_slice_in_dim(loads, first_row, row_count, 1)
    local_rows = first_row + jnp.arange(row_count, dtype=jnp.int32)
    pick_left = (left_rows[:, :, None] == local_rows[None, None, :]).astype(jnp.bfloat16)
    pick_right = (right_rows[:, :, None] == local_rows[None, None, :]).astype(jnp.bfloat16)
    first_local = jnp.einsum(
        "sij,sjc->sic", local_inverse, loads, preferred_element_type=jnp.float32
    )
    first_pass = precondition(first_local, loads_rows, coarse_basis, coarse_inverse, coarse_index)
    image_first = apply_stiffness(first_pass, stiffness, pick_left, pick_right)
    residual_b = (loads_rows.astype(jnp.float32) - image_first).astype(jnp.bfloat16)
    second_local = fold_product(
        local_inverse, lax.all_gather(residual_b, ("crow", "ccol"), axis=1, tiled=True)
    )
    second_pass = first_pass + precondition(
        second_local, residual_b, coarse_basis, coarse_inverse, coarse_index
    )
    image_second = apply_stiffness(second_pass, stiffness, pick_left, pick_right)
    final_residual = loads_rows.astype(jnp.float32) - image_second
    return (second_pass, final_residual)


def solution(mesh):
    return jax.shard_map(
        body,
        mesh=mesh,
        in_specs=(
            P("sub", None, None),
            P("sub", ("crow", "ccol"), None),
            P("sub", ("crow", "ccol"), None),
            P("sub", ("crow", "ccol"), None),
            P("sub", ("crow", "ccol")),
            P("sub", None),
            P("sub", None),
            P("sub", None),
        ),
        out_specs=(P("sub", ("crow", "ccol"), None), P("sub", ("crow", "ccol"), None)),
        check_vma=False,
    )
```

profile of v0, /device:TPU:1, one launch (start us, length us, event | category | flops | bytes accessed | tf_op | source)
XLA Modules:
  0.0 929.1 jit_solution(8455041256860478172)
XLA Ops:
  8.3 35.3 %psum.42 = bf16[2,48,128]{2,1,0:T(8,128)(2,1)} all-reduce(f32[2,48,128]{2,1,0:T(8,128)S(1)} %convolution_bitcast_fusion.4), channel_id=1, replica_groups=mesh['sub'=64,'crow'=4,'ccol'=2] {'crow','ccol'}, use_global_device_ids=true, to_apply=%region_0.0 | all-reduce | flops 12288 | bytes 73728 | tf_op jit(solution)/shard_map/psum | solution.py:77
  46.7 228.1 %all-reduce = s32[6144]{0:T(1024)S(1)} all-reduce(s32[6144]{0:T(1024)S(1)} %dynamic-update-slice), channel_id=1, replica_groups=mesh['sub'=64,'crow'=4,'ccol'=2] {'sub'}, use_global_device_ids=true, to_apply=%add | all-reduce | flops 6144 | bytes 49152
  274.8 16.2 %scatter_custom_fusion = bf16[769,128]{1,0:T(8,128)(2,1)S(1)} fusion(s32[6144]{0:T(1024)S(1)} %compare_select_fusion, bf16[6144,128]{1,0:T(8,128)(2,1)} %all-gather.5.cloned.1.call-done, bf16[]{:T(256)} %constant.10.clone.1), kind=kCustom, calls=%fused_computation.46 | custom fusion | bytes 197376 | tf_op jit(solution)/shard_map/scatter | solution.py:64
  292.1 84.9 %psum.43 = bf16[96,128]{1,0:T(8,128)(2,1)} all-reduce(f32[96,128]{1,0:T(8,128)S(1)} %convolution_bitcast_fusion.3), channel_id=1, replica_groups=mesh['sub'=64,'crow'=4,'ccol'=2] {'crow','ccol'}, use_global_device_ids=true, to_apply=%region_2.3 | all-reduce | flops 12288 | bytes 73728 | tf_op jit(solution)/shard_map/psum | solution.py:67
  377.8 71.1 %all-gather.7.cloned.1.call-done = bf16[6144,128]{1,0:T(8,128)(2,1)} async-done(((bf16[96,128]{1,0:T(8,128)(2,1)}), bf16[6144,128]{1,0:T(8,128)(2,1)}) %all-gather.7.cloned.1.call-update) | async-done | bytes 1572880 | tf_op jit(solution)/shard_map/all_gather | solution.py:68
  448.9 2.2 gather_fusion
  452.5 31.9 %all_gather.28 = bf16[2,1024,128]{2,1,0:T(8,128)(2,1)S(1)} all-gather(bf16[2,128,128]{2,1,0:T(8,128)(2,1)S(1)} %get-tuple-element.6), channel_id=1, replica_groups=mesh['sub'=64,'crow'=4,'ccol'=2] {'crow','ccol'}, dimensions={1}, use_global_device_ids=true | all-gather | bytes 589824 | tf_op jit(solution)/shard_map/all_gather | solution.py:28
  486.1 65.8 %all-reduce.4.cloned.1.call-done = bf16[2,2,128,128]{3,2,0,1:T(8,128)(2,1)} async-done(((bf16[2,2,128,128]{3,2,0,1:T(8,128)(2,1)}), bf16[2,2,128,128]{3,2,0,1:T(8,128)(2,1)}) %all-reduce.4.cloned.1.call-update) | async-done | bytes 131088 | tf_op jit(solution)/shard_map/psum | solution.py:35
  552.7 7.0 collective-permute-start.1
  559.7 1.9 collective-permute-start
  562.6 5.4 collective-permute-done
  569.2 32.8 %psum.45 = bf16[2,48,128]{2,1,0:T(8,128)(2,1)} all-reduce(f32[2,48,128]{2,1,0:T(8,128)S(1)} %convolution_bitcast_fusion.2), channel_id=1, replica_groups=mesh['sub'=64,'crow'=4,'ccol'=2] {'crow','ccol'}, use_global_device_ids=true, to_apply=%region_4.5 | all-reduce | flops 12288 | bytes 73728 | tf_op jit(solution)/shard_map/psum | solution.py:77
  602.0 72.8 %all-gather.9.cloned.1.call-done = bf16[6144,128]{1,0:T(8,128)(2,1)} async-done(((bf16[96,128]{1,0:T(8,128)(2,1)}), bf16[6144,128]{1,0:T(8,128)(2,1)}) %all-gather.9.cloned.1.call-update) | async-done | bytes 1572880 | tf_op jit(solution)/shard_map/all_gather | solution.py:55
  674.8 16.2 %scatter_custom_fusion.1 = bf16[769,128]{1,0:T(8,128)(2,1)S(1)} fusion(s32[6144]{0:T(1024)S(1)} %compare_select_fusion, bf16[6144,128]{1,0:T(8,128)(2,1)} %all-gather.9.cloned.1.call-done, bf16[]{:T(256)} %constant.10.clone.1), kind=kCustom, calls=%fused_computation.44 | custom fusion | bytes 197376 | tf_op jit(solution)/shard_map/scatter | solution.py:64
  691.2 35.8 %psum.46 = bf16[96,128]{1,0:T(8,128)(2,1)} all-reduce(f32[96,128]{1,0:T(8,128)S(1)} %convolution_bitcast_fusion.1), channel_id=1, replica_groups=mesh['sub'=64,'crow'=4,'ccol'=2] {'crow','ccol'}, use_global_device_ids=true, to_apply=%region_6.7 | all-reduce | flops 12288 | bytes 73728 | tf_op jit(solution)/shard_map/psum | solution.py:67
  727.1 27.2 %all_gather.29 = bf16[2,1024,128]{2,1,0:T(8,128)(2,1)S(1)} all-gather(bf16[2,128,128]{2,1,0:T(8,128)(2,1)S(1)} %fusion.6), channel_id=1, replica_groups=mesh['sub'=64,'crow'=4,'ccol'=2] {'crow','ccol'}, dimensions={1}, use_global_device_ids=true | all-gather | bytes 589824 | tf_op jit(solution)/shard_map/all_gather | solution.py:108
  754.3 47.3 %all-gather.11.cloned.1.call-done = bf16[6144,128]{1,0:T(8,128)(2,1)} async-done(((bf16[96,128]{1,0:T(8,128)(2,1)}), bf16[6144,128]{1,0:T(8,128)(2,1)}) %all-gather.11.cloned.1.call-update) | async-done | bytes 1572880 | tf_op jit(solution)/shard_map/all_gather | solution.py:68
  801.7 2.2 gather_fusion.1
  805.1 31.9 %all_gather.32 = bf16[2,1024,128]{2,1,0:T(8,128)(2,1)S(1)} all-gather(bf16[2,128,128]{2,1,0:T(8,128)(2,1)S(1)} %get-tuple-element.8), channel_id=1, replica_groups=mesh['sub'=64,'crow'=4,'ccol'=2] {'crow','ccol'}, dimensions={1}, use_global_device_ids=true | all-gather | bytes 589824 | tf_op jit(solution)/shard_map/all_gather | solution.py:28
  838.6 65.8 %all-reduce.6.cloned.1.call-done = bf16[2,2,128,128]{3,2,0,1:T(8,128)(2,1)} async-done(((bf16[2,2,128,128]{3,2,0,1:T(8,128)(2,1)}), bf16[2,2,128,128]{3,2,0,1:T(8,128)(2,1)}) %all-reduce.6.cloned.1.call-update) | async-done | bytes 131088 | tf_op jit(solution)/shard_map/psum | solution.py:35
  905.3 7.0 collective-permute-start.3
  912.3 1.9 collective-permute-start.2
  915.2 5.4 collective-permute-done.2
  920.6 1.6 fusion.3
  (59 shorter events, 16.1 us)
Async XLA Ops:
  7.2 445.0 %copy-start = (bf16[2,128,1024]{2,1,0:T(8,128)(2,1)S(1)}, bf16[2,128,1024]{2,1,0:T(8,128)(2,1)}, u32[]{:S(2)}) copy-start(bf16[2,128,1024]{2,1,0:T(8,128)(2,1)} %param.10) | copy-start | bytes 1572868
  7.2 445.0 %copy-start.2 = (bf16[2,1024,128]{2,1,0:T(8,128)(2,1)S(1)}, bf16[2,1024,128]{2,1,0:T(8,128)(2,1)}, u32[]{:S(2)}) copy-start(bf16[2,1024,128]{2,1,0:T(8,128)(2,1)} %param.8) | copy-start | bytes 1572868
  7.2 267.6 %all-gather.5.cloned.1.call-start = ((), (), s32[]{:S(2)}) async-start(), calls=%async_computation | async-start | bytes 1597440 | tf_op jit(solution)/shard_map/all_gather | solution.py:55
  43.6 405.3 %all-gather.7.cloned.1.call-start = ((), (), s32[]{:S(2)}) async-start(), calls=%async_computation.1 | async-start | bytes 1597440 | tf_op jit(solution)/shard_map/all_gather | solution.py:68
  274.7 209.7 %copy-start.1 = (bf16[2,128,1024]{2,1,0:T(8,128)(2,1)S(1)}, bf16[2,128,1024]{2,1,0:T(8,128)(2,1)}, u32[]{:S(2)}) copy-start(bf16[2,128,1024]{2,1,0:T(8,128)(2,1)} %param.9) | copy-start | bytes 1572868
  377.0 174.8 %all-reduce.4.cloned.1.call-start = ((), (), s32[]{:S(2)}) async-start(), calls=%async_computation.2 | async-start | bytes 262144 | tf_op jit(solution)/shard_map/psum | solution.py:35
  452.1 32.6 %copy-start.5 = (s32[2,128]{1,0:T(2,128)S(1)}, s32[2,128]{1,0:T(2,128)}, u32[]{:S(2)}) copy-start(s32[2,128]{1,0:T(2,128)} %param.15) | copy-start | bytes 3076
  452.2 32.9 %copy-start.6 = (s32[2,128]{1,0:T(2,128)S(1)}, s32[2,128]{1,0:T(2,128)}, u32[]{:S(2)}) copy-start(s32[2,128]{1,0:T(2,128)} %param.14) | copy-start | bytes 3076
  484.4 84.6 %copy-start.4 = (bf16[2,128,48]{1,2,0:T(8,128)(2,1)S(1)}, bf16[2,128,48]{1,2,0:T(8,128)(2,1)}, u32[]{:S(2)}) copy-start(bf16[2,128,48]{1,2,0:T(8,128)(2,1)} %param.11) | copy-start | bytes 73732
  484.4 206.5 %copy-start.3 = (bf16[96,768]{1,0:T(8,128)(2,1)S(1)}, bf16[96,768]{1,0:T(8,128)(2,1)}, u32[]{:S(2)}) copy-start(bf16[96,768]{1,0:T(8,128)(2,1)} %param.12) | copy-start | bytes 442372
  486.0 188.8 %all-gather.9.cloned.1.call-start = ((), (), s32[]{:S(2)}) async-start(), calls=%async_computation.3 | async-start | bytes 1597440 | tf_op jit(solution)/shard_map/all_gather | solution.py:55
  552.7 8.9 collective-permute-start.1
  559.7 8.3 collective-permute-start
  602.0 199.7 %all-gather.11.cloned.1.call-start = ((), (), s32[]{:S(2)}) async-start(), calls=%async_computation.4 | async-start | bytes 1597440 | tf_op jit(solution)/shard_map/all_gather | solution.py:68
  727.0 177.4 %all-reduce.6.cloned.1.call-start = ((), (), s32[]{:S(2)}) async-start(), calls=%async_computation.5 | async-start | bytes 262144 | tf_op jit(solution)/shard_map/psum | solution.py:35
  905.3 8.9 collective-permute-start.3
  912.3 8.3 collective-permute-start.2
Sparse Core Ops, SparseCore 0:
  43.8 79.1 all-gather.4
  377.1 71.7 all-gather.6
  486.1 65.6 all-reduce.3
  602.1 72.6 all-gather.8
  727.1 74.4 all-gather.10
  838.7 65.6 all-reduce.5
where the time goes:
time: 931 us; the launch traced here: 929 us
  blocking collectives  508 us (55%)
  waiting for transfers between devices  334 us (36%)
  local copies, waits for them, and re-layouts  41.7 us (4%)
  starting transfers between devices  18.1 us (2%)
  between operations  15 us (2%)
  matrix products  11.2 us (1%)
    unnamed x1, blocking collectives  228 us
    psum x2, waiting for transfers between devices, apply_stiffness(): boundary = lax.psum(partial_faces.astype(jnp.bfloat16), ('crow', 'ccol'))  132 us
    psum x2, blocking collectives, coarse_step(): coarse = lax.psum(partial_coarse, ('crow', 'ccol')).astype(jnp.bfloat16)  121 us
    all_gather x2, waiting for transfers between devices, coarse_step(): everything = lax.all_gather(coarse, 'sub', axis=0, tiled=True)  118 us
    all_gather x2, waiting for transfers between devices, coarse_step(): lax.all_gather(flat_rows, 'sub', axis=0, tiled=True)  72.8 us
    psum x2, blocking collectives, precondition(): restricted = lax.psum(partial_modes, ('crow', 'ccol')).astype(jnp.bfloat16)  68.1 us
    all_gather x2, blocking collectives, apply_stiffness(): lax.all_gather(rounded, ('crow', 'ccol'), axis=1, tiled=True)  63.9 us
    scatter x2, local copies, waits for them, and re-layouts, coarse_step(): ordered = jnp.zeros((block_width + 1, case_count), jnp.bfloat16).at[arriv...  32.4 us
  transfers between devices with their start and end apart: 10, of which 7 were waited for; matrix products, arithmetic and copies ran while one was open for 1% of the time, Pallas kernels for 0%

commit v1 on v0

v1 whole, which is shorter than its diff:
```python
import jax
import jax.numpy as jnp
from jax import lax
from jax.experimental import pallas as pl
from jax.experimental.pallas import tpu as pltpu
from jax.sharding import PartitionSpec as P

MESH = pl.DeviceIdType.MESH
F32, BF16, I32 = jnp.float32, jnp.bfloat16, jnp.int32
GROUP = 8
PLANE = 64
SIDE = 8
CAP = 24
SLOT = 32
BLOCK = 768
OWN = 96
PART = 12
STEP = 16
STAGES = ("place", "a", "b", "c", "d", "e", "v", "z", "before", "after", "r")


def dot(a, b):
    return jnp.dot(a, b, preferred_element_type=F32)


def dot_nt(a, b):
    return lax.dot_general(a, b, (((1,), (1,)), ((), ())), preferred_element_type=F32)


def kernel(
    loads, stiff, linv, basis, cinv, index_row, left, right,
    out_u, out_r,
    place_buf, cinv_wide, cinv_perm, bp, bext, pick_face, put_face, pick_coarse,
    sa, ra, gb, sc, rc, gd, re, pk, vb, zb, fs, nb, rf, local, first,
    send_sem, recv_sem,
):
    sub = lax.axis_index("sub")
    crow = lax.axis_index("crow")
    ccol = lax.axis_index("ccol")
    g = crow * 2 + ccol
    sy, sz = sub // SIDE, lax.rem(sub, SIDE)

    def group_peer(k):
        t = lax.rem(g + k, GROUP)
        return t, {"sub": sub, "crow": t // 2, "ccol": lax.rem(t, 2)}

    def plane_peer(k):
        y = lax.rem(sy + k // SIDE, SIDE)
        z = lax.rem(sz + lax.rem(k, SIDE), SIDE)
        return {"sub": y * SIDE + z, "crow": crow, "ccol": ccol}

    def line_peer(k):
        return {"sub": lax.rem(sub + k, PLANE), "crow": crow, "ccol": ccol}

    def sem_of(stage, p):
        i = STAGES.index(stage) * 2 + p
        return send_sem.at[i], recv_sem.at[i]

    def start(src, dst, stage, p, device):
        s, r = sem_of(stage, p)
        pltpu.make_async_remote_copy(
            src_ref=src, dst_ref=dst, send_sem=s, recv_sem=r, device_id=device, device_id_type=MESH
        ).start()

    def wait(ref, sem):
        pltpu.make_async_copy(ref, ref, sem).wait()

    def to_group(ref_of, dst, stage, p):
        def step(k, carry):
            t, device = group_peer(k)
            start(ref_of(t), dst, stage, p, device)
            return carry

        lax.fori_loop(1, GROUP, step, 0)

    def to_plane(ref, stage, p):
        def step(k, carry):
            start(ref, ref, stage, p, plane_peer(k))
            return carry

        lax.fori_loop(1, PLANE, step, 0)

    mine = pl.ds(pl.multiple_of(g * 128, 128), 128)

    for p in range(2):
        gb[p] = jnp.zeros(gb.shape[1:], BF16)
    pk[...] = jnp.zeros(pk.shape, BF16)

    barrier = pltpu.get_barrier_semaphore()

    def greet_group(k, carry):
        pl.semaphore_signal(barrier, inc=1, device_id=group_peer(k)[1], device_id_type=MESH)
        return carry

    def greet_plane(k, carry):
        pl.semaphore_signal(barrier, inc=1, device_id=plane_peer(k), device_id_type=MESH)
        return carry

    lax.fori_loop(1, GROUP, greet_group, 0)
    lax.fori_loop(1, PLANE, greet_plane, 0)

    lane = lax.broadcasted_iota(I32, (128, 128), 1).astype(F32)
    down = lax.broadcasted_iota(I32, (128, 128), 0).astype(F32)
    g_f = g.astype(F32)

    index_lane = jnp.broadcast_to(index_row[...].astype(F32), (128, 128))
    index_down = jnp.transpose(index_lane)

    def block_of(index):
        block = jnp.zeros(index.shape, F32)
        for t in range(1, GROUP):
            block += (index >= t * BLOCK).astype(F32)
        return jnp.where(index < 0, 99.0, block)

    block_lane, block_down = block_of(index_lane), block_of(index_down)
    earlier = (block_lane == block_down) & (down < lane)
    rank = jnp.sum(earlier.astype(F32), axis=0, keepdims=True)
    code_lane = jnp.broadcast_to(block_lane[0:1] * SLOT + rank, (128, 128))
    code_down = jnp.transpose(code_lane)
    select = jnp.concatenate(
        [(code_lane == down).astype(F32), (code_lane == down + 128.0).astype(F32)], axis=0
    ).astype(BF16)
    for s in range(2):
        k48 = lax.broadcasted_iota(I32, (48, 128), 0)
        l48 = lax.broadcasted_iota(I32, (48, 128), 1)
        shift = (l48 == k48 + 48 * s).astype(F32).astype(BF16)
        bext[s] = dot(basis[s], shift).astype(BF16)
        bp[s] = dot_nt(select, bext[s]).astype(BF16)

    slot = lane - SLOT * lax.rem(sub, 4).astype(F32)
    hit = (code_down == g_f * SLOT + slot) & (slot >= 0) & (slot < SLOT)
    place = jnp.sum(jnp.where(hit, index_down - g_f * BLOCK + 1.0, 0.0), axis=0, keepdims=True)
    place_buf[sub] = place

    def restrict(rows):
        part = dot(bp[0], rows[0]) + dot(bp[1], rows[1])
        return part.reshape(GROUP, SLOT, 128)

    sa[0] = restrict([loads[s, mine] for s in range(2)])

    pl.semaphore_wait(barrier, GROUP + PLANE - 2)

    def exchange_restricted(p):
        ra[p, g] = sa[p, g]
        to_group(
            lambda t: sa.at[p, t, pl.ds(0, CAP)], ra.at[p, g, pl.ds(0, CAP)], "a", p
        )

    def spread_restricted(p):
        wait(ra.at[p, pl.ds(0, GROUP - 1), pl.ds(0, CAP)], sem_of("a", p)[1])
        total = ra[p, 0, 0:CAP]
        for t in range(1, GROUP):
            total += ra[p, t, 0:CAP]
        gb[p, sub, 0:CAP] = total.astype(BF16)
        to_plane(gb.at[p, sub, pl.ds(0, CAP)], "b", p)

    exchange_restricted(0)
    to_plane(place_buf.at[sub], "place", 0)

    for s in range(2):
        local[s] = dot(linv[s], loads[s])
    spread_restricted(0)

    wide = (
        lax.broadcasted_iota(I32, (128, OWN), 1)
        == (lax.broadcasted_iota(I32, (128, OWN), 0) // STEP) * PART
        + lax.rem(lax.broadcasted_iota(I32, (128, OWN), 0), STEP)
    ) & (lax.rem(lax.broadcasted_iota(I32, (128, OWN), 0), STEP) < PART)
    cinv_wide[...] = dot(wide.astype(F32).astype(BF16), cinv[...]).astype(BF16)

    for s in range(2):
        for side, rows in enumerate((left, right)):
            row_lane = jnp.broadcast_to(rows[s : s + 1, :].astype(F32), (128, 128))
            row_down = jnp.transpose(row_lane)
            for j in range(8):
                pick_face[s, side, :, j * 128 : (j + 1) * 128] = (
                    (row_down == lane + 128.0 * j).astype(F32).astype(BF16)
                )
            put_face[s, side] = (row_lane == down + 128.0 * g_f).astype(F32).astype(BF16)
    for j in range(8):
        column = lax.broadcasted_iota(I32, (128, 128), 1) + 128 * j
        within = lax.rem(column, STEP)
        row_of = jnp.where(within < PART, (column // STEP) * OWN + PART * g + within, -5)
        pick_coarse[:, j * 128 : (j + 1) * 128] = (
            (index_down == row_of.astype(F32)).astype(F32).astype(BF16)
        )

    wait(place_buf.at[pl.ds(0, PLANE - 1)], sem_of("place", 0)[1])
    tall = lax.broadcasted_iota(I32, (BLOCK, 128), 0).astype(F32) + 1.0

    def permute(c, carry):
        spot = (
            place_buf[4 * c] + place_buf[4 * c + 1] + place_buf[4 * c + 2] + place_buf[4 * c + 3]
        )
        chosen = (tall == spot).astype(F32).astype(BF16)
        cinv_perm[:, pl.ds(pl.multiple_of(c * 128, 128), 128)] = dot(
            cinv_wide[...], chosen
        ).astype(BF16)
        return carry

    lax.fori_loop(0, PLANE // 4, permute, 0)

    def coarse(p):
        wait(gb.at[p, pl.ds(0, PLANE - 1), pl.ds(0, CAP)], sem_of("b", p)[1])
        part = dot(cinv_perm[...], gb[p].reshape(PLANE * SLOT, 128))
        sc[p] = part.reshape(GROUP, STEP, 128)
        rc[p, g] = sc[p, g]
        to_group(lambda t: sc.at[p, t], rc.at[p, g], "c", p)
        wait(rc.at[p, pl.ds(0, GROUP - 1)], sem_of("c", p)[1])
        total = rc[p, 0]
        for t in range(1, GROUP):
            total += rc[p, t]
        gd[p, sub] = total.astype(BF16)
        to_plane(gd.at[p, sub], "d", p)
        wait(gd.at[p, pl.ds(0, PLANE - 1)], sem_of("d", p)[1])
        found = dot(pick_coarse[...], gd[p].reshape(PLANE * STEP, 128))
        re[p, g] = found[0:OWN].astype(BF16)
        to_group(lambda t: re.at[p, g], re.at[p, g], "e", p)
        wait(re.at[p, pl.ds(0, GROUP - 1)], sem_of("e", p)[1])
        picked = re[p, 0].astype(F32)
        for t in range(1, GROUP):
            picked += re[p, t].astype(F32)
        pk[p, 0:OWN] = picked.astype(BF16)
        return [dot(bext[s], pk[p]) for s in range(2)]

    def apply(p, iterate):
        for s in range(2):
            vb[p, s, mine] = iterate[s].astype(BF16)
        to_group(lambda t: vb.at[p, :, mine], vb.at[p, :, mine], "v", p)
        wait(vb.at[p, :, pl.ds(0, 896)], sem_of("v", p)[1])
        image = []
        for s in range(2):
            z = dot(stiff[s], vb[p, s]).astype(BF16)
            zb[p, s, mine] = z
            image.append(z.astype(F32))
        to_group(lambda t: zb.at[p, :, mine], zb.at[p, :, mine], "z", p)
        wait(zb.at[p, :, pl.ds(0, 896)], sem_of("z", p)[1])
        fs[p, 0] = dot(pick_face[0, 0], zb[p, 0]).astype(BF16)
        fs[p, 1] = dot(pick_face[1, 1], zb[p, 1]).astype(BF16)
        start(fs.at[p, 0], nb.at[p, 1], "after", p, line_peer(PLANE - 1))
        start(fs.at[p, 1], nb.at[p, 0], "before", p, line_peer(1))
        to_one = dot(pick_face[0, 1], zb[p, 0]).astype(BF16)
        to_zero = dot(pick_face[1, 0], zb[p, 1]).astype(BF16)
        image[0] = image[0] + dot(put_face[0, 1], to_zero)
        image[1] = image[1] + dot(put_face[1, 0], to_one)
        wait(nb.at[p, 0], sem_of("before", p)[1])
        wait(nb.at[p, 1], sem_of("after", p)[1])
        image[0] = image[0] + dot(put_face[0, 0], nb[p, 0])
        image[1] = image[1] + dot(put_face[1, 1], nb[p, 1])
        return [loads[s, mine].astype(F32) - image[s] for s in range(2)]

    correction = coarse(0)
    for s in range(2):
        first[s] = local[s] + correction[s]
    residual = apply(0, [first[s] for s in range(2)])

    for s in range(2):
        rf[s, mine] = residual[s].astype(BF16)
    sa[1] = restrict([rf[s, mine] for s in range(2)])
    exchange_restricted(1)
    to_group(lambda t: rf.at[:, mine], rf.at[:, mine], "r", 0)
    spread_restricted(1)
    wait(rf.at[:, pl.ds(0, 896)], sem_of("r", 0)[1])
    for s in range(2):
        local[s] = dot(linv[s], rf[s])
    correction = coarse(1)
    for s in range(2):
        out_u[s] = first[s] + (local[s] + correction[s])
    final = apply(1, [out_u[s] for s in range(2)])
    for s in range(2):
        out_r[s] = final[s]

    wait(place_buf.at[pl.ds(0, PLANE - 1)], sem_of("place", 0)[0])
    wait(rf.at[:, pl.ds(0, 896)], sem_of("r", 0)[0])
    for p in range(2):
        wait(ra.at[p, pl.ds(0, GROUP - 1), pl.ds(0, CAP)], sem_of("a", p)[0])
        wait(gb.at[p, pl.ds(0, PLANE - 1), pl.ds(0, CAP)], sem_of("b", p)[0])
        wait(rc.at[p, pl.ds(0, GROUP - 1)], sem_of("c", p)[0])
        wait(gd.at[p, pl.ds(0, PLANE - 1)], sem_of("d", p)[0])
        wait(re.at[p, pl.ds(0, GROUP - 1)], sem_of("e", p)[0])
        wait(vb.at[p, :, pl.ds(0, 896)], sem_of("v", p)[0])
        wait(zb.at[p, :, pl.ds(0, 896)], sem_of("z", p)[0])
        wait(nb.at[p, 0], sem_of("before", p)[0])
        wait(nb.at[p, 1], sem_of("after", p)[0])


def body(loads, stiffness, local_inverse, coarse_basis, coarse_inverse, coarse_index, left, right):
    index_row = jnp.pad(coarse_index.reshape(1, OWN), ((0, 0), (0, 128 - OWN)), constant_values=-1)
    vmem = pl.BlockSpec(memory_space=pltpu.VMEM)
    out = jax.ShapeDtypeStruct((2, 128, 128), F32)
    count = 2 * len(STAGES)
    return pl.pallas_call(
        kernel,
        out_shape=(out, out),
        in_specs=[vmem] * 8,
        out_specs=(vmem, vmem),
        scratch_shapes=[
            pltpu.VMEM((PLANE, 1, 128), F32),
            pltpu.VMEM((128, BLOCK), BF16),
            pltpu.VMEM((128, PLANE * SLOT), BF16),
            pltpu.VMEM((2, GROUP * SLOT, 128), BF16),
            pltpu.VMEM((2, 128, 128), BF16),
            pltpu.VMEM((2, 2, 128, 1024), BF16),
            pltpu.VMEM((2, 2, 128, 128), BF16),
            pltpu.VMEM((128, PLANE * STEP), BF16),
            pltpu.VMEM((2, GROUP, SLOT, 128), F32),
            pltpu.VMEM((2, GROUP, SLOT, 128), F32),
            pltpu.VMEM((2, PLANE, SLOT, 128), BF16),
            pltpu.VMEM((2, GROUP, STEP, 128), F32),
            pltpu.VMEM((2, GROUP, STEP, 128), F32),
            pltpu.VMEM((2, PLANE, STEP, 128), BF16),
            pltpu.VMEM((2, GROUP, OWN, 128), BF16),
            pltpu.VMEM((2, 128, 128), BF16),
            pltpu.VMEM((2, 2, 1024, 128), BF16),
            pltpu.VMEM((2, 2, 1024, 128), BF16),
            pltpu.VMEM((2, 2, 128, 128), BF16),
            pltpu.VMEM((2, 2, 128, 128), BF16),
            pltpu.VMEM((2, 1024, 128), BF16),
            pltpu.VMEM((2, 128, 128), F32),
            pltpu.VMEM((2, 128, 128), F32),
            pltpu.SemaphoreType.DMA((count,)),
            pltpu.SemaphoreType.DMA((count,)),
        ],
        compiler_params=pltpu.CompilerParams(collective_id=0, has_side_effects=True),
        name="schwarz",
    )(loads, stiffness, local_inverse, coarse_basis, coarse_inverse, index_row, left, right)


def solution(mesh):
    group = ("crow", "ccol")
    return jax.shard_map(
        body,
        mesh=mesh,
        in_specs=(
            P("sub", None, None),
            P("sub", group, None),
            P("sub", group, None),
            P("sub", group, None),
            P("sub", group),
            P("sub", None),
            P("sub", None),
            P("sub", None),
        ),
        out_specs=(P("sub", group, None), P("sub", group, None)),
        check_vma=False,
    )
```

time: 931 us -> 142 us (0.15)
  blocking collectives: 508 us -> 0 us
  waiting for transfers between devices: 334 us -> 0 us
  Pallas kernels: 0 us -> 136 us
  local copies, waits for them, and re-layouts: 41.7 us -> 5.01 us
  starting transfers between devices: 18.1 us -> 0 us
  between operations: 15 us -> 0.65 us
  matrix products: 11.2 us -> 0 us
    unnamed x1 -> x0, blocking collectives: 228 us -> none
    all_gather x4 -> x0, waiting for transfers between devices: 191 us -> none  [the longest x2 118 us: coarse_step(): everything = lax.all_gather(coarse, 'sub', axis=0, tiled=True)]
    psum x4 -> x0, blocking collectives: 189 us -> none  [the longest x2 121 us: coarse_step(): coarse = lax.psum(partial_coarse, ('crow', 'ccol')).astype(jnp.bfloat16)]
    pallas_call x0 -> x1, Pallas kernels: none -> 136 us  [body(): pl.pallas_call(kernel, out_shape=(out, out), in_specs=[vmem] * 8, out_spe...]
    psum x2 -> x0, waiting for transfers between devices: 132 us -> none  [apply_stiffness(): boundary = lax.psum(partial_faces.astype(jnp.bfloat16), ('crow', 'ccol'))]
    all_gather x3 -> x0, blocking collectives: 91.1 us -> none  [the longest x2 63.9 us: apply_stiffness(): lax.all_gather(rounded, ('crow', 'ccol'), axis=1, tiled=True)]
    scatter x2 -> x0, local copies, waits for them, and re-layouts: 32.4 us -> none  [coarse_step(): ordered = jnp.zeros((block_width + 1, case_count), jnp.bfloat16).at[arriv...]
    ppermute x4 -> x0, starting transfers between devices: 17.9 us -> none  [the longest x2 14 us: padded(): lax.ppermute(lax.slice_in_dim(block, 0, width, axis=dim), axis, backward)]
  transfers between devices with their start and end apart: 10 -> 0, of which waited for: 7 -> 0; matrix products, arithmetic and copies ran while one was open for 1% -> 0% of each run, Pallas kernels for 0% -> 0%
where the time goes in v1:
time: 142 us; the launch traced here: 141 us
  Pallas kernels  136 us (96%)
  local copies, waits for them, and re-layouts  5.01 us (4%)
    pallas_call x1, Pallas kernels, body(): pl.pallas_call(kernel, out_shape=(out, out), in_specs=[vmem] * 8, out_spe...  136 us
    unnamed x5, local copies, waits for them, and re-layouts  3.73 us

profile of v1, /device:TPU:1, one launch (start us, length us, event | category | flops | bytes accessed | tf_op | source)
XLA Modules:
  0.0 141.4 jit_solution(17674345485611955662)
XLA Ops:
  0.6 0.8 reshape.7
  1.4 0.5 pad.4.index_row
  1.9 1.5 %copy.10.basis = bf16[2,128,48]{2,1,0:T(8,128)(2,1)} copy(bf16[2,128,48]{1,2,0:T(8,128)(2,1)} %param.11) | data formatting | bytes 49152 | tf_op args[3]
  3.4 135.7 %schwarz.1 = (f32[2,128,128]{2,1,0:T(8,128)}, f32[2,128,128]{2,1,0:T(8,128)}) custom-call(bf16[2,1024,128]{2,1,0:T(8,128)(2,1)} %loads.1, bf16[2,128,1024]{2,1,0:T(8,128)(2,1)} %stiff.1, bf16[2,128,1024]{2,1,0:T(8,128)(2,1)} %linv.1, bf16[2,128,48]{2,1,0:T(8,128)(2,1)} %copy.10.basis, bf16[96,768]{1,0:T(8,128)(2,1)} %cinv.1, s32[1,128]{1,0:T(1,128)} %pad.4.index_row, ...), custom_call_target="tpu_custom_call" | custom-call | tf_op jit(solution)/shard_map/schwarz/pallas_call | solution.py:292
  139.1 0.0 copy-start
  139.1 1.6 %copy.13 = f32[2,128,128]{2,1,0:T(8,128)} copy(f32[2,128,128]{2,1,0:T(8,128)} %get-tuple-element.4) | data formatting | bytes 262144
  140.7 0.0 copy-done
  140.7 0.7 copy.14
Async XLA Ops:
  139.1 1.6 %copy-start = (f32[2,128,128]{2,1,0:T(8,128)S(1)}, f32[2,128,128]{2,1,0:T(8,128)}, u32[]{:S(2)}) copy-start(f32[2,128,128]{2,1,0:T(8,128)} %get-tuple-element.5) | copy-start | bytes 393220

commit v2 on v1

v2 whole, which is shorter than its diff:
```python
import jax
import jax.numpy as jnp
from jax import lax
from jax.experimental import pallas as pl
from jax.experimental.pallas import tpu as pltpu
from jax.sharding import PartitionSpec as P

MESH = pl.DeviceIdType.MESH
F32, BF16, I32 = jnp.float32, jnp.bfloat16, jnp.int32
GROUP = 8
PLANE = 64
SIDE = 8
CAP = 24
HEAD, TAIL = 16, 8
BLOCK = 768
OWN = 96
MODES = 48
STEP = 16
STAGES = ("basis", "faces", "a", "c", "d", "e", "w", "r", "inner", "before", "after")
PIPES = ("place", "b0", "b1")
NEAREST = (1, 7, 2, 6, 3, 5, 4)


def dot(a, b):
    return jnp.dot(a, b, preferred_element_type=F32)


def dot_tn(a, b):
    return lax.dot_general(a, b, (((0,), (0,)), ((), ())), preferred_element_type=F32)


def mask(condition):
    return condition.astype(F32).astype(BF16)


def iota(shape, dim):
    return lax.broadcasted_iota(I32, shape, dim)


def kernel(
    loads_in, stiff_in, linv_in, basis, cinv_in, index_in, left, right,
    out_u, out_r,
    loads, stiff, linv, cinv,
    place_buf, cinv_wide, perm_head, perm_tail, bp, basis_t, basis_full, put_face, pick_coarse,
    face_part, face_got, face_own, sa, ra, head, tail, sc, rc, gd, re, pk, wb, vb, fs, nb, rf, local, first, restricted,
    send_sem, recv_sem, near_recv, far_recv, near_send, far_send, load_sem,
):
    sub = lax.axis_index("sub")
    crow = lax.axis_index("crow")
    ccol = lax.axis_index("ccol")
    core = lax.rem(crow, 2)
    chip = (crow // 2) * 2 + ccol
    g = crow * 2 + ccol
    sy, sz = sub // SIDE, lax.rem(sub, SIDE)
    q1 = sz * (1 - core) + sy * core
    q2 = sy * (1 - core) + sz * core

    def group_peer(k):
        t = lax.rem(g + k, GROUP)
        return t, {"sub": sub, "crow": t // 2, "ccol": lax.rem(t, 2)}

    def plane_at(a, b):
        y = b * (1 - core) + a * core
        z = a * (1 - core) + b * core
        return {"sub": y * SIDE + z, "crow": crow, "ccol": ccol}

    def first_peer(d):
        return plane_at(lax.rem(q1 + d, SIDE), q2)

    def second_peer(d):
        return plane_at(q1, lax.rem(q2 + d, SIDE))

    def plane_peer(k):
        y = lax.rem(sy + k // SIDE, SIDE)
        z = lax.rem(sz + lax.rem(k, SIDE), SIDE)
        return {"sub": y * SIDE + z, "crow": crow, "ccol": ccol}

    def copy(src, dst, s, r, device):
        pltpu.make_async_remote_copy(
            src_ref=src, dst_ref=dst, send_sem=s, recv_sem=r, device_id=device, device_id_type=MESH
        ).start()

    def wait(ref, sem):
        pltpu.make_async_copy(ref, ref, sem).wait()

    def repeat(low, high, step):
        def one(k, carry):
            step(k)
            return carry

        lax.fori_loop(low, high, one, 0)

    def sems(stage, p):
        i = STAGES.index(stage) * 2 + p
        return send_sem.at[i], recv_sem.at[i]

    def to_group(ref_of, dst, stage, p):
        s, r = sems(stage, p)

        def step(k):
            t, device = group_peer(k)
            copy(ref_of(t), dst, s, r, device)

        repeat(1, GROUP, step)

    mine = pl.ds(pl.multiple_of(g * 128, 128), 128)
    seven = pl.ds(0, 7)

    arrivals = {
        "basis": lambda p: basis_t.at[:, pl.ds(0, 896)],
        "faces": lambda p: face_got.at[seven],
        "a": lambda p: ra.at[seven],
        "c": lambda p: rc.at[p, seven],
        "e": lambda p: re.at[p, seven],
        "w": lambda p: wb.at[p, :, pl.ds(0, 896)],
        "r": lambda p: rf.at[:, pl.ds(0, 896)],
        "inner": lambda p: nb.at[p, pl.ds(0, 2), seven],
        "before": lambda p: nb.at[p, 2],
        "after": lambda p: nb.at[p, 3],
    }

    def arrived(stage, p):
        wait(arrivals[stage](p), sems(stage, p)[1])

    def spot(half):
        return (q2, q1) if half == 0 else (q1, q2)

    def near_peer(half, d):
        return first_peer(d) if half == 0 else second_peer(d)

    def far_peer(half, d):
        return second_peer(d) if half == 0 else first_peer(d)

    def pipe_start(name, refs):
        i = PIPES.index(name)

        def near(d):
            for half, ref in enumerate(refs):
                block = ref.at[spot(half)]
                copy(block, block, near_send.at[i, half], near_recv.at[i, half, d], near_peer(half, d))

        def far(d):
            for half, ref in enumerate(refs):
                block = ref.at[spot(half)]
                copy(block, block, far_send.at[i, half], far_recv.at[i, half], far_peer(half, d))

        repeat(1, SIDE, near)
        repeat(1, SIDE, far)

    def pipe_forward(name, refs):
        i = PIPES.index(name)
        for e in NEAREST:
            for half, ref in enumerate(refs):
                a, b = spot(half)
                block = ref.at[a, lax.rem(b + SIDE - e, SIDE)]
                wait(block, near_recv.at[i, half, e])

                def far(d):
                    copy(block, block, far_send.at[i, half], far_recv.at[i, half], far_peer(half, d))

                repeat(1, SIDE, far)

    def pipe_wait(name, refs):
        i = PIPES.index(name)
        for half, ref in enumerate(refs):
            wait(ref.at[seven], far_recv.at[i, half])

    def pipe_settle(name, refs):
        i = PIPES.index(name)
        for half, ref in enumerate(refs):
            wait(ref.at[0, seven], near_send.at[i, half])
            wait(ref.at[seven], far_send.at[i, half])

    gd[...] = jnp.zeros(gd.shape, BF16)
    pk[...] = jnp.zeros(pk.shape, BF16)

    barrier = pltpu.get_barrier_semaphore()

    def greet(k):
        for device in (group_peer(k)[1], first_peer(k), second_peer(k)):
            pl.semaphore_signal(barrier, inc=1, device_id=device, device_id_type=MESH)

    repeat(1, SIDE, greet)

    operands = ((stiff_in, stiff), (linv_in, linv), (loads_in, loads), (cinv_in, cinv))
    for i, (outer, inner) in enumerate(operands):
        pltpu.make_async_copy(outer, inner, load_sem.at[i]).start()

    lane_i, down_i = iota((128, 128), 1), iota((128, 128), 0)
    lane, down = lane_i.astype(F32), down_i.astype(F32)
    g_f = g.astype(F32)

    index_lane = jnp.zeros((8, 128), F32)
    for s in range(2):
        shift = mask(iota((MODES, 128), 1) == iota((MODES, 128), 0) + MODES * s)
        index = jnp.broadcast_to(index_in[s : s + 1, :], (8, MODES))
        high = lax.shift_right_logical(index, 6)
        low = index - high * 64
        index_lane += 64.0 * dot(high.astype(F32).astype(BF16), shift)
        index_lane += dot(low.astype(F32).astype(BF16), shift)
    index_lane = jnp.broadcast_to(index_lane[0:1], (128, 128))
    index_lane = jnp.where(lane < OWN, index_lane, -1.0)
    index_down = jnp.transpose(index_lane)

    def block_of(index):
        block = jnp.zeros(index.shape, F32)
        for t in range(1, GROUP):
            block += (index >= t * BLOCK).astype(F32)
        return jnp.where(index < 0, 99.0, block)

    block_lane, block_down = block_of(index_lane), block_of(index_down)
    earlier = (block_lane == block_down) & (down < lane)
    rank = jnp.sum(earlier.astype(F32), axis=0, keepdims=True)
    code_lane = jnp.broadcast_to(block_lane[0:1] * CAP + rank, (128, 128))
    code_down = jnp.transpose(code_lane)
    select_own = mask(code_lane[0:CAP] == down[0:CAP] + g_f * CAP)

    slot = lane - (q1 * HEAD).astype(F32)
    in_head = (code_down == g_f * CAP + slot) & (slot >= 0) & (slot < HEAD)
    slot = lane - (lax.rem(q1, 2) * 64 + q2 * TAIL).astype(F32)
    in_tail = (code_down == g_f * CAP + HEAD + slot) & (slot >= 0) & (slot < TAIL)
    value = index_down - g_f * BLOCK + 1.0
    place_buf[q2, q1, :, 0:128] = jnp.sum(jnp.where(in_head, value, 0.0), axis=0, keepdims=True)
    place_buf[q2, q1, :, 128:256] = jnp.sum(jnp.where(in_tail, value, 0.0), axis=0, keepdims=True)

    basis_own = basis[...].reshape(OWN, 128)
    basis_t[:, mine] = basis_own

    pl.semaphore_wait(barrier, GROUP + 2 * SIDE - 3)

    to_group(lambda t: basis_t.at[:, mine], basis_t.at[:, mine], "basis", 0)
    pipe_start("place", [place_buf])

    for i, (outer, inner) in enumerate(operands):
        pltpu.make_async_copy(outer, inner, load_sem.at[i]).wait()
    for s in range(2):
        for side, rows in enumerate((left, right)):
            row_lane = jnp.broadcast_to(rows[s : s + 1, :].astype(F32), (128, 128))
            put = row_lane == down + 128.0 * g_f
            put_face[s, side] = mask(put)
            pick = mask(jnp.transpose(put.astype(F32)) > 0.5)
            part = dot(pick, stiff[s]).astype(BF16)
            face_part[:, (2 * s + side) * STEP : (2 * s + side + 1) * STEP, :] = part.reshape(
                GROUP, STEP, 1024
            )

    def settle_faces():
        total = face_got[0]
        for t in range(1, GROUP):
            total += face_got[t]
        face_own[...] = total

    arrived("basis", 0)
    for s in range(2):
        restricted[s * MODES : (s + 1) * MODES] = dot(
            basis_t[s * MODES : (s + 1) * MODES, :], loads[s]
        ).astype(BF16)
    rows = dot(select_own[:, 0:OWN], restricted[...]).astype(BF16)

    def spread(p, rows):
        head[(p, *spot(0))] = rows[0:HEAD]
        tail[(p, *spot(1))] = rows[HEAD:CAP]
        pipe_start(PIPES[1 + p], [head.at[p], tail.at[p]])

    spread(0, rows)
    face_got[g] = face_part[g]
    to_group(lambda t: face_part.at[t], face_got.at[g], "faces", 0)
    pipe_forward("place", [place_buf])
    pipe_forward("b0", [head.at[0], tail.at[0]])

    out_row, out_of = iota((128, OWN), 0), iota((128, OWN), 1)
    part_of, within = out_row // STEP, lax.rem(out_row, STEP)
    part_core = lax.rem(part_of // 2, 2)
    part_chip = (part_of // 4) * 2 + lax.rem(part_of, 2)
    wide = (out_of == part_chip * CAP + part_core * STEP + within) & (within < STEP - 8 * part_core)
    cinv_wide[...] = dot(mask(wide), cinv[...]).astype(BF16)
    for j in range(8):
        column = lane_i + 128 * j
        within = lax.rem(column, STEP)
        row_of = (column // STEP) * OWN + chip * CAP + core * STEP + within
        row_of = jnp.where(within < STEP - 8 * core, row_of, -5)
        pick_coarse[:, j * 128 : (j + 1) * 128] = mask(index_down == row_of.astype(F32))[0:OWN]
    for s in range(2):
        for j in range(8):
            shift = mask(iota((MODES, 128), 1) == iota((MODES, 128), 0) + MODES * s)
            turned = dot_tn(basis_t[s * MODES : (s + 1) * MODES, j * 128 : (j + 1) * 128], shift)
            basis_full[s, j * 128 : (j + 1) * 128, :] = turned.astype(BF16)
    select = mask(
        jnp.broadcast_to(code_lane[0:1], (GROUP * CAP, 128)) == iota((GROUP * CAP, 128), 0).astype(F32)
    )
    for s in range(2):
        keep = (iota((OWN, 128), 0) >= s * MODES) & (iota((OWN, 128), 0) < (s + 1) * MODES)
        part = jnp.where(keep, basis_own.astype(F32), 0.0).astype(BF16)
        bp[s] = dot(select[:, 0:OWN], part).astype(BF16)

    pipe_wait("place", [place_buf])
    tall = iota((BLOCK, 128), 0).astype(F32) + 1.0
    for c in range(8):
        where = jnp.sum(place_buf[c, :, 0, 0:128], axis=0, keepdims=True)
        perm_head[:, c * 128 : (c + 1) * 128] = dot(cinv_wide[...], mask(tall == where)).astype(BF16)
    for c in range(4):
        where = jnp.sum(
            place_buf[:, 2 * c, 0, 128:256] + place_buf[:, 2 * c + 1, 0, 128:256], axis=0, keepdims=True
        )
        perm_tail[:, c * 128 : (c + 1) * 128] = dot(cinv_wide[...], mask(tall == where)).astype(BF16)
    for s in range(2):
        local[s] = dot(linv[s], loads[s])
        wb[0, s, mine] = local[s].astype(BF16)

    def coarse_start(p):
        pipe_wait(PIPES[1 + p], [head.at[p], tail.at[p]])
        part = dot(perm_head[...], head[p].reshape(PLANE * HEAD, 128))
        part += dot(perm_tail[...], tail[p].reshape(PLANE * TAIL, 128))
        sc[p] = part.reshape(GROUP, STEP, 128)
        rc[p, g] = sc[p, g]
        to_group(lambda t: sc.at[p, t], rc.at[p, g], "c", p)
        arrived("c", p)
        total = rc[p, 0]
        for t in range(1, GROUP):
            total += rc[p, t]
        gd[p, sub] = total.astype(BF16)
        s, r = sems("d", p)
        for kind, size in enumerate((16, 8)):
            @pl.when(core == kind)
            def _():
                block = gd.at[p, sub, pl.ds(0, size)]
                repeat(1, PLANE, lambda k: copy(block, block, s, r, plane_peer(k)))

    def each_plane(p, which):
        for kind, size in enumerate((16, 8)):
            @pl.when(core == kind)
            def _():
                wait(gd.at[p, pl.ds(0, PLANE - 1), pl.ds(0, size)], sems("d", p)[which])

    def coarse_end(p):
        each_plane(p, 1)
        found = dot(pick_coarse[...], gd[p].reshape(PLANE * STEP, 128))
        re[p, g] = found.astype(BF16)
        to_group(lambda t: re.at[p, g], re.at[p, g], "e", p)
        arrived("e", p)
        picked = re[p, 0].astype(F32)
        for t in range(1, GROUP):
            picked += re[p, t].astype(F32)
        pk[p, 0:OWN] = picked.astype(BF16)

    def apply(p):
        arrived("w", p)
        for s in range(2):
            vb[s] = (wb[p, s].astype(F32) + dot(basis_full[s], pk[p])).astype(BF16)
        faces = [dot(face_own[2 * STEP * s : 2 * STEP * (s + 1)], vb[s]).astype(BF16) for s in range(2)]
        nb[p, 0, g] = faces[1][0:STEP]
        nb[p, 1, g] = faces[0][STEP : 2 * STEP]
        fs[p, 0] = faces[0][0:STEP]
        fs[p, 1] = faces[1][STEP : 2 * STEP]
        s_before, r_before = sems("before", p)
        s_after, r_after = sems("after", p)

        def outward(k):
            t = lax.rem(g + k, GROUP)
            place = {"crow": t // 2, "ccol": lax.rem(t, 2)}
            up = {"sub": lax.rem(sub + 1, PLANE), **place}
            low = {"sub": lax.rem(sub + PLANE - 1, PLANE), **place}
            copy(fs.at[p, 1], nb.at[p, 2, g], s_before, r_before, up)
            copy(fs.at[p, 0], nb.at[p, 3, g], s_after, r_after, low)

        repeat(0, GROUP, outward)
        inner = nb.at[p, pl.ds(0, 2), g]
        to_group(lambda t: inner, inner, "inner", p)
        image = [dot(stiff[s], vb[s]).astype(BF16).astype(F32) for s in range(2)]
        arrived("inner", p)
        image[0] += dot(put_face[0, 1], nb[p, 0].reshape(128, 128))
        image[1] += dot(put_face[1, 0], nb[p, 1].reshape(128, 128))
        arrived("before", p)
        image[0] += dot(put_face[0, 0], nb[p, 2].reshape(128, 128))
        arrived("after", p)
        image[1] += dot(put_face[1, 1], nb[p, 3].reshape(128, 128))
        return [loads[s, mine].astype(F32) - image[s] for s in range(2)]

    coarse_start(0)
    to_group(lambda t: wb.at[0, :, mine], wb.at[0, :, mine], "w", 0)
    arrived("faces", 0)
    settle_faces()
    coarse_end(0)
    for s in range(2):
        first[s] = local[s] + dot(basis_full[s, mine], pk[0])
    residual = apply(0)

    for s in range(2):
        rf[s, mine] = residual[s].astype(BF16)
    part = dot(bp[0], rf[0, mine]) + dot(bp[1], rf[1, mine])
    sa[...] = part.reshape(GROUP, CAP, 128)
    ra[g] = sa[g]
    to_group(lambda t: sa.at[t], ra.at[g], "a", 0)
    arrived("a", 0)
    total = ra[0]
    for t in range(1, GROUP):
        total += ra[t]
    spread(1, total.astype(BF16))
    to_group(lambda t: rf.at[:, mine], rf.at[:, mine], "r", 0)
    pipe_forward("b1", [head.at[1], tail.at[1]])
    arrived("r", 0)
    for s in range(2):
        local[s] = dot(linv[s], rf[s])
        wb[1, s, mine] = (first[s] + local[s]).astype(BF16)
    coarse_start(1)
    to_group(lambda t: wb.at[1, :, mine], wb.at[1, :, mine], "w", 1)
    coarse_end(1)
    for s in range(2):
        out_u[s] = first[s] + (local[s] + dot(basis_full[s, mine], pk[1]))
    final = apply(1)
    for s in range(2):
        out_r[s] = final[s]

    for stage in ("basis", "faces", "a", "r"):
        wait(arrivals[stage](0), sems(stage, 0)[0])
    pipe_settle("place", [place_buf])
    for p in range(2):
        for stage in ("c", "e", "w", "inner", "before", "after"):
            wait(arrivals[stage](p), sems(stage, p)[0])
        each_plane(p, 0)
        pipe_settle(PIPES[1 + p], [head.at[p], tail.at[p]])


def body(loads, stiffness, local_inverse, coarse_basis, coarse_inverse, coarse_index, left, right):
    vmem = pl.BlockSpec(memory_space=pltpu.VMEM)
    away = pl.BlockSpec(memory_space=pl.ANY)
    out = jax.ShapeDtypeStruct((2, 128, 128), F32)
    count = 2 * len(STAGES)
    dma = pltpu.SemaphoreType.DMA
    return pl.pallas_call(
        kernel,
        out_shape=(out, out),
        in_specs=[away, away, away, vmem, away, vmem, vmem, vmem],
        out_specs=(vmem, vmem),
        scratch_shapes=[
            pltpu.VMEM((2, 1024, 128), BF16),
            pltpu.VMEM((2, 128, 1024), BF16),
            pltpu.VMEM((2, 128, 1024), BF16),
            pltpu.VMEM((OWN, BLOCK), BF16),
            pltpu.VMEM((SIDE, SIDE, 1, 256), F32),
            pltpu.VMEM((128, BLOCK), BF16),
            pltpu.VMEM((128, PLANE * HEAD), BF16),
            pltpu.VMEM((128, PLANE * TAIL), BF16),
            pltpu.VMEM((2, GROUP * CAP, 128), BF16),
            pltpu.VMEM((OWN, 1024), BF16),
            pltpu.VMEM((2, 1024, 128), BF16),
            pltpu.VMEM((2, 2, 128, 128), BF16),
            pltpu.VMEM((OWN, PLANE * STEP), BF16),
            pltpu.VMEM((GROUP, 4 * STEP, 1024), BF16),
            pltpu.VMEM((GROUP, 4 * STEP, 1024), BF16),
            pltpu.VMEM((4 * STEP, 1024), BF16),
            pltpu.VMEM((GROUP, CAP, 128), F32),
            pltpu.VMEM((GROUP, CAP, 128), F32),
            pltpu.VMEM((2, SIDE, SIDE, HEAD, 128), BF16),
            pltpu.VMEM((2, SIDE, SIDE, TAIL, 128), BF16),
            pltpu.VMEM((2, GROUP, STEP, 128), F32),
            pltpu.VMEM((2, GROUP, STEP, 128), F32),
            pltpu.VMEM((2, PLANE, STEP, 128), BF16),
            pltpu.VMEM((2, GROUP, OWN, 128), BF16),
            pltpu.VMEM((2, 128, 128), BF16),
            pltpu.VMEM((2, 2, 1024, 128), BF16),
            pltpu.VMEM((2, 1024, 128), BF16),
            pltpu.VMEM((2, 2, STEP, 128), BF16),
            pltpu.VMEM((2, 4, GROUP, STEP, 128), BF16),
            pltpu.VMEM((2, 1024, 128), BF16),
            pltpu.VMEM((2, 128, 128), F32),
            pltpu.VMEM((2, 128, 128), F32),
            pltpu.VMEM((OWN, 128), BF16),
            dma((count,)),
            dma((count,)),
            dma((len(PIPES), 2, SIDE)),
            dma((len(PIPES), 2)),
            dma((len(PIPES), 2)),
            dma((len(PIPES), 2)),
            dma((4,)),
        ],
        compiler_params=pltpu.CompilerParams(collective_id=0, has_side_effects=True),
        name="schwarz",
    )(
        loads, stiffness, local_inverse, jnp.swapaxes(coarse_basis, 1, 2), coarse_inverse, coarse_index, left, right
    )


def solution(mesh):
    group = ("crow", "ccol")
    return jax.shard_map(
        body,
        mesh=mesh,
        in_specs=(
            P("sub", None, None),
            P("sub", group, None),
            P("sub", group, None),
            P("sub", group, None),
            P("sub", group),
            P("sub", None),
            P("sub", None),
            P("sub", None),
        ),
        out_specs=(P("sub", group, None), P("sub", group, None)),
        check_vma=False,
    )
```

time: 142 us -> 98.9 us (0.70)
  Pallas kernels: 136 us -> 95.7 us
  local copies, waits for them, and re-layouts: 5.01 us -> 2.26 us
    pallas_call x1, Pallas kernels: 136 us -> 95.7 us  [body(): pl.pallas_call(kernel, out_shape=(out, out), in_specs=[away, away, away,...]
    unnamed x5 -> x4, local copies, waits for them, and re-layouts: 3.73 us -> 2.26 us
where the time goes in v2:
time: 98.9 us; the launch traced here: 98.7 us
  Pallas kernels  95.7 us (97%)
  local copies, waits for them, and re-layouts  2.26 us (2%)
    pallas_call x1, Pallas kernels, body(): pl.pallas_call(kernel, out_shape=(out, out), in_specs=[away, away, away,...  95.7 us
    unnamed x4, local copies, waits for them, and re-layouts  2.26 us

profile of v2, /device:TPU:1, one launch (start us, length us, event | category | flops | bytes accessed | tf_op | source)
XLA Modules:
  0.0 98.7 jit_solution(6464838663658298590)
XLA Ops:
  0.6 95.7 %schwarz.1 = (f32[2,128,128]{2,1,0:T(8,128)}, f32[2,128,128]{2,1,0:T(8,128)}) custom-call(bf16[2,1024,128]{2,1,0:T(8,128)(2,1)} %loads_in.1, bf16[2,128,1024]{2,1,0:T(8,128)(2,1)} %stiff_in.1, bf16[2,128,1024]{2,1,0:T(8,128)(2,1)} %linv_in.1, bf16[2,48,128]{2,1,0:T(8,128)(2,1)} %bitcast.1, bf16[96,768]{1,0:T(8,128)(2,1)} %cinv_in.1, s32[2,48]{1,0:T(2,128)} %index_in.1, ...), custom_call_target="tpu_custom_call" | custom-call | tf_op jit(solution)/shard_map/schwarz/pallas_call | solution.py:430
  96.4 0.0 copy-start
  96.4 1.6 %copy.12 = f32[2,128,128]{2,1,0:T(8,128)} copy(f32[2,128,128]{2,1,0:T(8,128)} %get-tuple-element.4) | data formatting | bytes 262144
  98.0 0.0 copy-done
  98.0 0.7 copy.13
Async XLA Ops:
  96.4 1.6 %copy-start = (f32[2,128,128]{2,1,0:T(8,128)S(1)}, f32[2,128,128]{2,1,0:T(8,128)}, u32[]{:S(2)}) copy-start(f32[2,128,128]{2,1,0:T(8,128)} %get-tuple-element.5) | copy-start | bytes 393220

commit v3 on v2

--- a/solution.py
+++ b/solution.py
@@ -42,7 +42,7 @@
     out_u, out_r,
     loads, stiff, linv, cinv,
     place_buf, cinv_wide, perm_head, perm_tail, bp, basis_t, basis_full, put_face, pick_coarse,
-    face_part, face_got, face_own, sa, ra, head, tail, sc, rc, gd, re, pk, wb, vb, fs, nb, rf, local, first, restricted,
+    face_part, face_got, face_own, sa, ra, head, tail, sc, rc, gd, re, pk, wb, ab, fs, nb, rf, local, first, kept, restricted,
     send_sem, recv_sem, near_recv, far_recv, near_send, far_send, load_sem,
 ):
     sub = lax.axis_index("sub")
@@ -70,9 +70,12 @@
     def second_peer(d):
         return plane_at(q1, lax.rem(q2 + d, SIDE))
 
+    def far_first(i):
+        return 4 + (1 - 2 * lax.rem(i, 2)) * ((i + 1) // 2)
+
     def plane_peer(k):
-        y = lax.rem(sy + k // SIDE, SIDE)
-        z = lax.rem(sz + lax.rem(k, SIDE), SIDE)
+        y = lax.rem(sy + far_first(k // SIDE), SIDE)
+        z = lax.rem(sz + far_first(lax.rem(k, SIDE)), SIDE)
         return {"sub": y * SIDE + z, "crow": crow, "ccol": ccol}
 
     def copy(src, dst, s, r, device):
@@ -105,6 +108,9 @@
 
     mine = pl.ds(pl.multiple_of(g * 128, 128), 128)
     seven = pl.ds(0, 7)
+
+    def kinds(p):
+        return pl.ds(0, 2) if p == 0 else pl.ds(2, 1)
 
     arrivals = {
         "basis": lambda p: basis_t.at[:, pl.ds(0, 896)],
@@ -114,9 +120,9 @@
         "e": lambda p: re.at[p, seven],
         "w": lambda p: wb.at[p, :, pl.ds(0, 896)],
         "r": lambda p: rf.at[:, pl.ds(0, 896)],
-        "inner": lambda p: nb.at[p, pl.ds(0, 2), seven],
-        "before": lambda p: nb.at[p, 2],
-        "after": lambda p: nb.at[p, 3],
+        "inner": lambda p: nb.at[kinds(p), pl.ds(0, 2), seven],
+        "before": lambda p: nb.at[kinds(p), 2],
+        "after": lambda p: nb.at[kinds(p), 3],
     }
 
     def arrived(stage, p):
@@ -144,8 +150,8 @@
                 block = ref.at[spot(half)]
                 copy(block, block, far_send.at[i, half], far_recv.at[i, half], far_peer(half, d))
 
-        repeat(1, SIDE, near)
-        repeat(1, SIDE, far)
+        repeat(0, SIDE - 1, lambda k: near(far_first(k)))
+        repeat(0, SIDE - 1, lambda k: far(far_first(k)))
 
     def pipe_forward(name, refs):
         i = PIPES.index(name)
@@ -158,7 +164,7 @@
                 def far(d):
                     copy(block, block, far_send.at[i, half], far_recv.at[i, half], far_peer(half, d))
 
-                repeat(1, SIDE, far)
+                repeat(0, SIDE - 1, lambda k: far(far_first(k)))
 
     def pipe_wait(name, refs):
         i = PIPES.index(name)
@@ -222,6 +228,7 @@
     value = index_down - g_f * BLOCK + 1.0
     place_buf[q2, q1, :, 0:128] = jnp.sum(jnp.where(in_head, value, 0.0), axis=0, keepdims=True)
     place_buf[q2, q1, :, 128:256] = jnp.sum(jnp.where(in_tail, value, 0.0), axis=0, keepdims=True)
+    place_buf[q2, q1, :, 256:384] = index_lane[0:1]
 
     basis_own = basis[...].reshape(OWN, 128)
     basis_t[:, mine] = basis_own
@@ -244,54 +251,41 @@
                 GROUP, STEP, 1024
             )
 
-    def settle_faces():
-        total = face_got[0]
-        for t in range(1, GROUP):
-            total += face_got[t]
-        face_own[...] = total
-
-    arrived("basis", 0)
-    for s in range(2):
-        restricted[s * MODES : (s + 1) * MODES] = dot(
-            basis_t[s * MODES : (s + 1) * MODES, :], loads[s]
-        ).astype(BF16)
-    rows = dot(select_own[:, 0:OWN], restricted[...]).astype(BF16)
-
-    def spread(p, rows):
-        head[(p, *spot(0))] = rows[0:HEAD]
-        tail[(p, *spot(1))] = rows[HEAD:CAP]
-        pipe_start(PIPES[1 + p], [head.at[p], tail.at[p]])
-
-    spread(0, rows)
-    face_got[g] = face_part[g]
-    to_group(lambda t: face_part.at[t], face_got.at[g], "faces", 0)
-    pipe_forward("place", [place_buf])
-    pipe_forward("b0", [head.at[0], tail.at[0]])
-
     out_row, out_of = iota((128, OWN), 0), iota((128, OWN), 1)
     part_of, within = out_row // STEP, lax.rem(out_row, STEP)
     part_core = lax.rem(part_of // 2, 2)
     part_chip = (part_of // 4) * 2 + lax.rem(part_of, 2)
     wide = (out_of == part_chip * CAP + part_core * STEP + within) & (within < STEP - 8 * part_core)
     cinv_wide[...] = dot(mask(wide), cinv[...]).astype(BF16)
-    for j in range(8):
-        column = lane_i + 128 * j
-        within = lax.rem(column, STEP)
-        row_of = (column // STEP) * OWN + chip * CAP + core * STEP + within
-        row_of = jnp.where(within < STEP - 8 * core, row_of, -5)
-        pick_coarse[:, j * 128 : (j + 1) * 128] = mask(index_down == row_of.astype(F32))[0:OWN]
-    for s in range(2):
-        for j in range(8):
-            shift = mask(iota((MODES, 128), 1) == iota((MODES, 128), 0) + MODES * s)
-            turned = dot_tn(basis_t[s * MODES : (s + 1) * MODES, j * 128 : (j + 1) * 128], shift)
-            basis_full[s, j * 128 : (j + 1) * 128, :] = turned.astype(BF16)
-    select = mask(
-        jnp.broadcast_to(code_lane[0:1], (GROUP * CAP, 128)) == iota((GROUP * CAP, 128), 0).astype(F32)
-    )
-    for s in range(2):
-        keep = (iota((OWN, 128), 0) >= s * MODES) & (iota((OWN, 128), 0) < (s + 1) * MODES)
-        part = jnp.where(keep, basis_own.astype(F32), 0.0).astype(BF16)
-        bp[s] = dot(select[:, 0:OWN], part).astype(BF16)
+    for s in range(2):
+        local[s] = dot(linv[s], loads[s])
+        wb[0, s, mine] = local[s].astype(BF16)
+
+
+    def settle_faces():
+        total = face_got[0]
+        for t in range(1, GROUP):
+            total += face_got[t]
+        face_own[...] = total
+
+    arrived("basis", 0)
+    for s in range(2):
+        restricted[s * MODES : (s + 1) * MODES] = dot(
+            basis_t[s * MODES : (s + 1) * MODES, :], loads[s]
+        ).astype(BF16)
+    rows = dot(select_own[:, 0:OWN], restricted[...]).astype(BF16)
+
+    def spread(p, rows):
+        head[(p, *spot(0))] = rows[0:HEAD]
+        tail[(p, *spot(1))] = rows[HEAD:CAP]
+        pipe_start(PIPES[1 + p], [head.at[p], tail.at[p]])
+
+    spread(0, rows)
+    face_got[g] = face_part[g]
+    to_group(lambda t: face_part.at[t], face_got.at[g], "faces", 0)
+    to_group(lambda t: wb.at[0, :, mine], wb.at[0, :, mine], "w", 0)
+    pipe_forward("place", [place_buf])
+    pipe_forward("b0", [head.at[0], tail.at[0]])
 
     pipe_wait("place", [place_buf])
     tall = iota((BLOCK, 128), 0).astype(F32) + 1.0
@@ -304,8 +298,36 @@
         )
         perm_tail[:, c * 128 : (c + 1) * 128] = dot(cinv_wide[...], mask(tall == where)).astype(BF16)
     for s in range(2):
-        local[s] = dot(linv[s], loads[s])
-        wb[0, s, mine] = local[s].astype(BF16)
+        for j in range(8):
+            shift = mask(iota((MODES, 128), 1) == iota((MODES, 128), 0) + MODES * s)
+            turned = dot_tn(basis_t[s * MODES : (s + 1) * MODES, j * 128 : (j + 1) * 128], shift)
+            basis_full[s, j * 128 : (j + 1) * 128, :] = turned.astype(BF16)
+    select = mask(
+        jnp.broadcast_to(code_lane[0:1], (GROUP * CAP, 128)) == iota((GROUP * CAP, 128), 0).astype(F32)
+    )
+    for s in range(2):
+        keep = (iota((OWN, 128), 0) >= s * MODES) & (iota((OWN, 128), 0) < (s + 1) * MODES)
+        part = jnp.where(keep, basis_own.astype(F32), 0.0).astype(BF16)
+        bp[s] = dot(select[:, 0:OWN], part).astype(BF16)
+
+    def index_of(other):
+        y, z = other // SIDE, lax.rem(other, SIDE)
+        a = z * (1 - core) + y * core
+        b = y * (1 - core) + z * core
+        return place_buf[b, a, :, 256:384]
+
+    after_index = index_of(lax.rem(sub + 1, PLANE))
+    before_index = index_of(lax.rem(sub + PLANE - 1, PLANE))
+    index_near = jnp.where(lane[0:1] < MODES, after_index, before_index)
+    index_near = jnp.transpose(jnp.broadcast_to(index_near, (128, 128)))
+    for j in range(8):
+        column = lane_i + 128 * j
+        within = lax.rem(column, STEP)
+        row_of = (column // STEP) * OWN + chip * CAP + core * STEP + within
+        row_of = jnp.where(within < STEP - 8 * core, row_of, -5)
+        for k, index in enumerate((index_down, index_near)):
+            chosen = mask(index == row_of.astype(F32))[0:OWN]
+            pick_coarse[k * OWN : (k + 1) * OWN, j * 128 : (j + 1) * 128] = chosen
 
     def coarse_start(p):
         pipe_wait(PIPES[1 + p], [head.at[p], tail.at[p]])
@@ -314,6 +336,11 @@
         sc[p] = part.reshape(GROUP, STEP, 128)
         rc[p, g] = sc[p, g]
         to_group(lambda t: sc.at[p, t], rc.at[p, g], "c", p)
+        if p == 0:
+            arrived("faces", 0)
+            settle_faces()
+            arrived("w", 0)
+            faces_start(0)
         arrived("c", p)
         total = rc[p, 0]
         for t in range(1, GROUP):
@@ -324,7 +351,7 @@
             @pl.when(core == kind)
             def _():
                 block = gd.at[p, sub, pl.ds(0, size)]
-                repeat(1, PLANE, lambda k: copy(block, block, s, r, plane_peer(k)))
+                repeat(0, PLANE - 1, lambda k: copy(block, block, s, r, plane_peer(k)))
 
     def each_plane(p, which):
         for kind, size in enumerate((16, 8)):
@@ -332,26 +359,30 @@
             def _():
                 wait(gd.at[p, pl.ds(0, PLANE - 1), pl.ds(0, size)], sems("d", p)[which])
 
-    def coarse_end(p):
+    def coarse_pick(p):
         each_plane(p, 1)
         found = dot(pick_coarse[...], gd[p].reshape(PLANE * STEP, 128))
         re[p, g] = found.astype(BF16)
         to_group(lambda t: re.at[p, g], re.at[p, g], "e", p)
+    def coarse_end(p):
         arrived("e", p)
         picked = re[p, 0].astype(F32)
         for t in range(1, GROUP):
             picked += re[p, t].astype(F32)
-        pk[p, 0:OWN] = picked.astype(BF16)
-
-    def apply(p):
-        arrived("w", p)
-        for s in range(2):
-            vb[s] = (wb[p, s].astype(F32) + dot(basis_full[s], pk[p])).astype(BF16)
-        faces = [dot(face_own[2 * STEP * s : 2 * STEP * (s + 1)], vb[s]).astype(BF16) for s in range(2)]
-        nb[p, 0, g] = faces[1][0:STEP]
-        nb[p, 1, g] = faces[0][STEP : 2 * STEP]
-        fs[p, 0] = faces[0][0:STEP]
-        fs[p, 1] = faces[1][STEP : 2 * STEP]
+        pk[p, 0, 0:OWN] = picked[0:OWN].astype(BF16)
+        pk[p, 1, 0:OWN] = picked[OWN : 2 * OWN].astype(BF16)
+
+
+    def faces_start(p):
+        for kind in range(2 * p, 2 + p):
+            source = basis_full if kind == 1 else wb.at[p]
+            faces = [
+                dot(face_own[2 * STEP * s : 2 * STEP * (s + 1)], source[s]).astype(BF16) for s in range(2)
+            ]
+            nb[kind, 0, g] = faces[1][0:STEP]
+            nb[kind, 1, g] = faces[0][STEP : 2 * STEP]
+            fs[kind, 0] = faces[0][0:STEP]
+            fs[kind, 1] = faces[1][STEP : 2 * STEP]
         s_before, r_before = sems("before", p)
         s_after, r_after = sems("after", p)
 
@@ -360,54 +391,82 @@
             place = {"crow": t // 2, "ccol": lax.rem(t, 2)}
             up = {"sub": lax.rem(sub + 1, PLANE), **place}
             low = {"sub": lax.rem(sub + PLANE - 1, PLANE), **place}
-            copy(fs.at[p, 1], nb.at[p, 2, g], s_before, r_before, up)
-            copy(fs.at[p, 0], nb.at[p, 3, g], s_after, r_after, low)
+            copy(fs.at[kinds(p), 1], nb.at[kinds(p), 2, g], s_before, r_before, up)
+            copy(fs.at[kinds(p), 0], nb.at[kinds(p), 3, g], s_after, r_after, low)
 
         repeat(0, GROUP, outward)
-        inner = nb.at[p, pl.ds(0, 2), g]
+        inner = nb.at[kinds(p), pl.ds(0, 2), g]
         to_group(lambda t: inner, inner, "inner", p)
-        image = [dot(stiff[s], vb[s]).astype(BF16).astype(F32) for s in range(2)]
-        arrived("inner", p)
-        image[0] += dot(put_face[0, 1], nb[p, 0].reshape(128, 128))
-        image[1] += dot(put_face[1, 0], nb[p, 1].reshape(128, 128))
-        arrived("before", p)
-        image[0] += dot(put_face[0, 0], nb[p, 2].reshape(128, 128))
-        arrived("after", p)
-        image[1] += dot(put_face[1, 1], nb[p, 3].reshape(128, 128))
-        return [loads[s, mine].astype(F32) - image[s] for s in range(2)]
+
+    def faces_wait(p):
+        for stage in ("inner", "before", "after"):
+            arrived(stage, p)
+
+    def face(kind, which):
+        return nb[kind, which].reshape(128, 128)
+
+    def residual_local(p):
+        kind = 2 * p
+        after = (face(kind, 0), face(kind, 3))
+        before = (face(kind, 2), face(kind, 1))
+        return [
+            loads[s, mine].astype(F32)
+            - (dot(stiff[s], wb[p, s]) + dot(put_face[s, 0], before[s]) + dot(put_face[s, 1], after[s]))
+            for s in range(2)
+        ]
+
+    def residual_of(p, early):
+        return [early[s] - (dot(ab[s, 0], pk[p, 0]) + dot(ab[s, 1], pk[p, 1])) for s in range(2)]
 
     coarse_start(0)
-    to_group(lambda t: wb.at[0, :, mine], wb.at[0, :, mine], "w", 0)
-    arrived("faces", 0)
-    settle_faces()
-    coarse_end(0)
-    for s in range(2):
-        first[s] = local[s] + dot(basis_full[s, mine], pk[0])
-    residual = apply(0)
-
-    for s in range(2):
-        rf[s, mine] = residual[s].astype(BF16)
-    part = dot(bp[0], rf[0, mine]) + dot(bp[1], rf[1, mine])
-    sa[...] = part.reshape(GROUP, CAP, 128)
+    faces_wait(0)
+    for s in range(2):
+        image = dot(stiff[s], basis_full[s])
+        if s == 0:
+            ab[s, 0] = (image + dot(put_face[0, 1], face(1, 0))).astype(BF16)
+            ab[s, 1] = dot(put_face[0, 0], face(1, 2)).astype(BF16)
+        else:
+            ab[s, 0] = (image + dot(put_face[1, 0], face(1, 1))).astype(BF16)
+            ab[s, 1] = dot(put_face[1, 1], face(1, 3)).astype(BF16)
+    early = residual_local(0)
+    for s in range(2):
+        kept[s] = early[s]
+    pieces = [[early[s].astype(BF16) for s in range(2)]] + [[ab[s, k] for s in range(2)] for k in range(2)]
+    for k, piece in enumerate(pieces):
+        part = dot(bp[0], piece[0]) + dot(bp[1], piece[1])
+        sa[:, k] = part.reshape(GROUP, CAP, 128)
     ra[g] = sa[g]
     to_group(lambda t: sa.at[t], ra.at[g], "a", 0)
+    coarse_pick(0)
     arrived("a", 0)
     total = ra[0]
     for t in range(1, GROUP):
         total += ra[t]
-    spread(1, total.astype(BF16))
+    coarse_end(0)
+    rows = total[0] - dot(total[1].astype(BF16), pk[0, 0]) - dot(total[2].astype(BF16), pk[0, 1])
+    spread(1, rows.astype(BF16))
+    residual = residual_of(0, [kept[s] for s in range(2)])
+    for s in range(2):
+        rf[s, mine] = residual[s].astype(BF16)
     to_group(lambda t: rf.at[:, mine], rf.at[:, mine], "r", 0)
+    for s in range(2):
+        first[s] = local[s] + dot(basis_full[s, mine], pk[0, 0])
     pipe_forward("b1", [head.at[1], tail.at[1]])
     arrived("r", 0)
     for s in range(2):
-        local[s] = dot(linv[s], rf[s])
-        wb[1, s, mine] = (first[s] + local[s]).astype(BF16)
+        first[s] = first[s] + dot(linv[s], rf[s])
+        wb[1, s, mine] = first[s].astype(BF16)
     coarse_start(1)
     to_group(lambda t: wb.at[1, :, mine], wb.at[1, :, mine], "w", 1)
+    arrived("w", 1)
+    faces_start(1)
+    coarse_pick(1)
+    faces_wait(1)
+    early = residual_local(1)
     coarse_end(1)
     for s in range(2):
-        out_u[s] = first[s] + (local[s] + dot(basis_full[s, mine], pk[1]))
-    final = apply(1)
+        out_u[s] = first[s] + dot(basis_full[s, mine], pk[1, 0])
+    final = residual_of(1, early)
     for s in range(2):
         out_r[s] = final[s]
 
@@ -437,7 +496,7 @@
             pltpu.VMEM((2, 128, 1024), BF16),
             pltpu.VMEM((2, 128, 1024), BF16),
             pltpu.VMEM((OWN, BLOCK), BF16),
-            pltpu.VMEM((SIDE, SIDE, 1, 256), F32),
+            pltpu.VMEM((SIDE, SIDE, 1, 384), F32),
             pltpu.VMEM((128, BLOCK), BF16),
             pltpu.VMEM((128, PLANE * HEAD), BF16),
             pltpu.VMEM((128, PLANE * TAIL), BF16),
@@ -445,24 +504,25 @@
             pltpu.VMEM((OWN, 1024), BF16),
             pltpu.VMEM((2, 1024, 128), BF16),
             pltpu.VMEM((2, 2, 128, 128), BF16),
-            pltpu.VMEM((OWN, PLANE * STEP), BF16),
+            pltpu.VMEM((2 * OWN, PLANE * STEP), BF16),
             pltpu.VMEM((GROUP, 4 * STEP, 1024), BF16),
             pltpu.VMEM((GROUP, 4 * STEP, 1024), BF16),
             pltpu.VMEM((4 * STEP, 1024), BF16),
-            pltpu.VMEM((GROUP, CAP, 128), F32),
-            pltpu.VMEM((GROUP, CAP, 128), F32),
+            pltpu.VMEM((GROUP, 3, CAP, 128), F32),
+            pltpu.VMEM((GROUP, 3, CAP, 128), F32),
             pltpu.VMEM((2, SIDE, SIDE, HEAD, 128), BF16),
             pltpu.VMEM((2, SIDE, SIDE, TAIL, 128), BF16),
             pltpu.VMEM((2, GROUP, STEP, 128), F32),
             pltpu.VMEM((2, GROUP, STEP, 128), F32),
             pltpu.VMEM((2, PLANE, STEP, 128), BF16),
-            pltpu.VMEM((2, GROUP, OWN, 128), BF16),
-            pltpu.VMEM((2, 128, 128), BF16),
+            pltpu.VMEM((2, GROUP, 2 * OWN, 128), BF16),
+            pltpu.VMEM((2, 2, 128, 128), BF16),
             pltpu.VMEM((2, 2, 1024, 128), BF16),
+            pltpu.VMEM((2, 2, 128, 128), BF16),
+            pltpu.VMEM((3, 2, STEP, 128), BF16),
+            pltpu.VMEM((3, 4, GROUP, STEP, 128), BF16),
             pltpu.VMEM((2, 1024, 128), BF16),
-            pltpu.VMEM((2, 2, STEP, 128), BF16),
-            pltpu.VMEM((2, 4, GROUP, STEP, 128), BF16),
-            pltpu.VMEM((2, 1024, 128), BF16),
+            pltpu.VMEM((2, 128, 128), F32),
             pltpu.VMEM((2, 128, 128), F32),
             pltpu.VMEM((2, 128, 128), F32),
             pltpu.VMEM((OWN, 128), BF16),

time: 98.9 us -> 95.8 us (0.969)
  Pallas kernels: 95.7 us -> 92.7 us
    pallas_call x1, Pallas kernels: 95.7 us -> 92.7 us  [body(): pl.pallas_call(kernel, out_shape=(out, out), in_specs=[away, away, away,...]
where the time goes in v3:
time: 95.8 us; the launch traced here: 95.6 us
  Pallas kernels  92.7 us (97%)
  local copies, waits for them, and re-layouts  2.26 us (2%)
    pallas_call x1, Pallas kernels, body(): pl.pallas_call(kernel, out_shape=(out, out), in_specs=[away, away, away,...  92.7 us
    unnamed x4, local copies, waits for them, and re-layouts  2.26 us

profile of v3, /device:TPU:1, one launch (start us, length us, event | category | flops | bytes accessed | tf_op | source)
XLA Modules:
  0.0 95.6 jit_solution(13910595148938424144)
XLA Ops:
  0.6 92.7 %schwarz.1 = (f32[2,128,128]{2,1,0:T(8,128)}, f32[2,128,128]{2,1,0:T(8,128)}) custom-call(bf16[2,1024,128]{2,1,0:T(8,128)(2,1)} %loads_in.1, bf16[2,128,1024]{2,1,0:T(8,128)(2,1)} %stiff_in.1, bf16[2,128,1024]{2,1,0:T(8,128)(2,1)} %linv_in.1, bf16[2,48,128]{2,1,0:T(8,128)(2,1)} %bitcast.1, bf16[96,768]{1,0:T(8,128)(2,1)} %cinv_in.1, s32[2,48]{1,0:T(2,128)} %index_in.1, ...), custom_call_target="tpu_custom_call" | custom-call | tf_op jit(solution)/shard_map/schwarz/pallas_call | solution.py:489
  93.3 0.0 copy-start
  93.3 1.6 %copy.12 = f32[2,128,128]{2,1,0:T(8,128)} copy(f32[2,128,128]{2,1,0:T(8,128)} %get-tuple-element.4) | data formatting | bytes 262144
  95.0 0.0 copy-done
  95.0 0.7 copy.13
Async XLA Ops:
  93.3 1.6 %copy-start = (f32[2,128,128]{2,1,0:T(8,128)S(1)}, f32[2,128,128]{2,1,0:T(8,128)}, u32[]{:S(2)}) copy-start(f32[2,128,128]{2,1,0:T(8,128)} %get-tuple-element.5) | copy-start | bytes 393220

commit v4 on v3

--- a/solution.py
+++ b/solution.py
@@ -16,7 +16,7 @@
 OWN = 96
 MODES = 48
 STEP = 16
-STAGES = ("basis", "faces", "a", "c", "d", "e", "w", "r", "inner", "before", "after")
+STAGES = ("basis", "pair", "faces", "a", "c", "d", "e", "w", "r", "inner", "before", "after")
 PIPES = ("place", "b0", "b1")
 NEAREST = (1, 7, 2, 6, 3, 5, 4)
 
@@ -42,7 +42,7 @@
     out_u, out_r,
     loads, stiff, linv, cinv,
     place_buf, cinv_wide, perm_head, perm_tail, bp, basis_t, basis_full, put_face, pick_coarse,
-    face_part, face_got, face_own, sa, ra, head, tail, sc, rc, gd, re, pk, wb, ab, fs, nb, rf, local, first, kept, restricted,
+    face_part, face_pair, face_got, face_own, sa, ra, head, tail, sc, rc, gd, re, pk, wb, ab, fs, nb, rf, local, first, kept, restricted,
     send_sem, recv_sem, near_recv, far_recv, near_send, far_send, load_sem,
 ):
     sub = lax.axis_index("sub")
@@ -114,7 +114,8 @@
 
     arrivals = {
         "basis": lambda p: basis_t.at[:, pl.ds(0, 896)],
-        "faces": lambda p: face_got.at[seven],
+        "pair": lambda p: face_pair,
+        "faces": lambda p: face_got.at[pl.ds(0, 3)],
         "a": lambda p: ra.at[seven],
         "c": lambda p: rc.at[p, seven],
         "e": lambda p: re.at[p, seven],
@@ -251,23 +252,41 @@
                 GROUP, STEP, 1024
             )
 
+    partner = {"sub": sub, "crow": crow + 1 - 2 * core, "ccol": ccol}
+    for half in range(2):
+        theirs = face_part.at[pl.ds(4 * half + 2 * (1 - core), 2)]
+        copy(theirs, face_pair.at[pl.ds(2 * half, 2)], *sems("pair", 0), partner)
+    for s in range(2):
+        local[s] = dot(linv[s], loads[s])
+        wb[0, s, mine] = local[s].astype(BF16)
+    to_group(lambda t: wb.at[0, :, mine], wb.at[0, :, mine], "w", 0)
     out_row, out_of = iota((128, OWN), 0), iota((128, OWN), 1)
     part_of, within = out_row // STEP, lax.rem(out_row, STEP)
     part_core = lax.rem(part_of // 2, 2)
     part_chip = (part_of // 4) * 2 + lax.rem(part_of, 2)
     wide = (out_of == part_chip * CAP + part_core * STEP + within) & (within < STEP - 8 * part_core)
     cinv_wide[...] = dot(mask(wide), cinv[...]).astype(BF16)
-    for s in range(2):
-        local[s] = dot(linv[s], loads[s])
-        wb[0, s, mine] = local[s].astype(BF16)
 
 
     def settle_faces():
-        total = face_got[0]
-        for t in range(1, GROUP):
-            total += face_got[t]
-        face_own[...] = total
-
+        face_own[...] = face_got[0] + face_got[1] + face_got[2] + face_got[3]
+
+    def pass_faces():
+        arrived("pair", 0)
+        for half in range(2):
+            ours = pl.ds(4 * half + 2 * core, 2)
+            face_part[ours] = face_part[ours] + face_pair[2 * half : 2 * half + 2]
+        face_got[chip] = face_part[g]
+
+        def step(k):
+            other = lax.rem(chip + k, 4)
+            row, column = (other // 2) * 2 + core, lax.rem(other, 2)
+            device = {"sub": sub, "crow": row, "ccol": column}
+            copy(face_part.at[row * 2 + column], face_got.at[chip], *sems("faces", 0), device)
+
+        repeat(1, 4, step)
+
+    pass_faces()
     arrived("basis", 0)
     for s in range(2):
         restricted[s * MODES : (s + 1) * MODES] = dot(
@@ -281,9 +300,6 @@
         pipe_start(PIPES[1 + p], [head.at[p], tail.at[p]])
 
     spread(0, rows)
-    face_got[g] = face_part[g]
-    to_group(lambda t: face_part.at[t], face_got.at[g], "faces", 0)
-    to_group(lambda t: wb.at[0, :, mine], wb.at[0, :, mine], "w", 0)
     pipe_forward("place", [place_buf])
     pipe_forward("b0", [head.at[0], tail.at[0]])
 
@@ -470,7 +486,7 @@
     for s in range(2):
         out_r[s] = final[s]
 
-    for stage in ("basis", "faces", "a", "r"):
+    for stage in ("basis", "pair", "faces", "a", "r"):
         wait(arrivals[stage](0), sems(stage, 0)[0])
     pipe_settle("place", [place_buf])
     for p in range(2):
@@ -506,7 +522,8 @@
             pltpu.VMEM((2, 2, 128, 128), BF16),
             pltpu.VMEM((2 * OWN, PLANE * STEP), BF16),
             pltpu.VMEM((GROUP, 4 * STEP, 1024), BF16),
-            pltpu.VMEM((GROUP, 4 * STEP, 1024), BF16),
+            pltpu.VMEM((4, 4 * STEP, 1024), BF16),
+            pltpu.VMEM((4, 4 * STEP, 1024), BF16),
             pltpu.VMEM((4 * STEP, 1024), BF16),
             pltpu.VMEM((GROUP, 3, CAP, 128), F32),
             pltpu.VMEM((GROUP, 3, CAP, 128), F32),

time: 95.8 us -> 88.4 us (0.923)
  Pallas kernels: 92.7 us -> 85.3 us
    pallas_call x1, Pallas kernels: 92.7 us -> 85.3 us  [body(): pl.pallas_call(kernel, out_shape=(out, out), in_specs=[away, away, away,...]
where the time goes in v4:
time: 88.4 us; the launch traced here: 88.2 us
  Pallas kernels  85.3 us (96%)
  local copies, waits for them, and re-layouts  2.26 us (3%)
    pallas_call x1, Pallas kernels, body(): pl.pallas_call(kernel, out_shape=(out, out), in_specs=[away, away, away,...  85.3 us
    unnamed x4, local copies, waits for them, and re-layouts  2.26 us

profile of v4, /device:TPU:1, one launch (start us, length us, event | category | flops | bytes accessed | tf_op | source)
XLA Modules:
  0.0 88.2 jit_solution(4846563169099907933)
XLA Ops:
  0.6 85.3 %schwarz.1 = (f32[2,128,128]{2,1,0:T(8,128)}, f32[2,128,128]{2,1,0:T(8,128)}) custom-call(bf16[2,1024,128]{2,1,0:T(8,128)(2,1)} %loads_in.1, bf16[2,128,1024]{2,1,0:T(8,128)(2,1)} %stiff_in.1, bf16[2,128,1024]{2,1,0:T(8,128)(2,1)} %linv_in.1, bf16[2,48,128]{2,1,0:T(8,128)(2,1)} %bitcast.1, bf16[96,768]{1,0:T(8,128)(2,1)} %cinv_in.1, s32[2,48]{1,0:T(2,128)} %index_in.1, ...), custom_call_target="tpu_custom_call" | custom-call | tf_op jit(solution)/shard_map/schwarz/pallas_call | solution.py:505
  85.9 0.0 copy-start
  85.9 1.6 %copy.12 = f32[2,128,128]{2,1,0:T(8,128)} copy(f32[2,128,128]{2,1,0:T(8,128)} %get-tuple-element.4) | data formatting | bytes 262144
  87.5 0.0 copy-done
  87.5 0.7 copy.13
Async XLA Ops:
  85.9 1.6 %copy-start = (f32[2,128,128]{2,1,0:T(8,128)S(1)}, f32[2,128,128]{2,1,0:T(8,128)}, u32[]{:S(2)}) copy-start(f32[2,128,128]{2,1,0:T(8,128)} %get-tuple-element.5) | copy-start | bytes 393220

commit v5 on v4

--- a/solution.py
+++ b/solution.py
@@ -38,9 +38,9 @@
 
 
 def kernel(
-    loads_in, stiff_in, linv_in, basis, cinv_in, index_in, left, right,
-    out_u, out_r,
-    loads, stiff, linv, cinv,
+    loads_in, stiff_in, linv_in, basis_in, cinv_in, index_in, left_in, right_in,
+    out,
+    loads, stiff, linv, cinv, index_own, basis, left, right,
     place_buf, cinv_wide, perm_head, perm_tail, bp, basis_t, basis_full, put_face, pick_coarse,
     face_part, face_pair, face_got, face_own, sa, ra, head, tail, sc, rc, gd, re, pk, wb, ab, fs, nb, rf, local, first, kept, restricted,
     send_sem, recv_sem, near_recv, far_recv, near_send, far_send, load_sem,
@@ -178,9 +178,6 @@
             wait(ref.at[0, seven], near_send.at[i, half])
             wait(ref.at[seven], far_send.at[i, half])
 
-    gd[...] = jnp.zeros(gd.shape, BF16)
-    pk[...] = jnp.zeros(pk.shape, BF16)
-
     barrier = pltpu.get_barrier_semaphore()
 
     def greet(k):
@@ -189,9 +186,17 @@
 
     repeat(1, SIDE, greet)
 
-    operands = ((stiff_in, stiff), (linv_in, linv), (loads_in, loads), (cinv_in, cinv))
+    operands = ((stiff_in, stiff), (linv_in, linv), (loads_in, loads), (cinv_in, cinv), (left_in, left), (right_in, right))
+    urgent = ((index_in, index_own), (basis_in, basis))
+    for i, (outer, inner) in enumerate(urgent):
+        pltpu.make_async_copy(outer, inner, load_sem.at[len(operands) + i]).start()
     for i, (outer, inner) in enumerate(operands):
         pltpu.make_async_copy(outer, inner, load_sem.at[i]).start()
+
+    gd[...] = jnp.zeros(gd.shape, BF16)
+    pk[...] = jnp.zeros(pk.shape, BF16)
+    for i, (outer, inner) in enumerate(urgent):
+        pltpu.make_async_copy(outer, inner, load_sem.at[len(operands) + i]).wait()
 
     lane_i, down_i = iota((128, 128), 1), iota((128, 128), 0)
     lane, down = lane_i.astype(F32), down_i.astype(F32)
@@ -200,7 +205,7 @@
     index_lane = jnp.zeros((8, 128), F32)
     for s in range(2):
         shift = mask(iota((MODES, 128), 1) == iota((MODES, 128), 0) + MODES * s)
-        index = jnp.broadcast_to(index_in[s : s + 1, :], (8, MODES))
+        index = jnp.broadcast_to(index_own[s : s + 1, :], (8, MODES))
         high = lax.shift_right_logical(index, 6)
         low = index - high * 64
         index_lane += 64.0 * dot(high.astype(F32).astype(BF16), shift)
@@ -474,17 +479,17 @@
         wb[1, s, mine] = first[s].astype(BF16)
     coarse_start(1)
     to_group(lambda t: wb.at[1, :, mine], wb.at[1, :, mine], "w", 1)
+    coarse_pick(1)
     arrived("w", 1)
     faces_start(1)
-    coarse_pick(1)
     faces_wait(1)
     early = residual_local(1)
     coarse_end(1)
     for s in range(2):
-        out_u[s] = first[s] + dot(basis_full[s, mine], pk[1, 0])
+        out[s] = first[s] + dot(basis_full[s, mine], pk[1, 0])
     final = residual_of(1, early)
     for s in range(2):
-        out_r[s] = final[s]
+        out[2 + s] = final[s]
 
     for stage in ("basis", "pair", "faces", "a", "r"):
         wait(arrivals[stage](0), sems(stage, 0)[0])
@@ -502,16 +507,20 @@
     out = jax.ShapeDtypeStruct((2, 128, 128), F32)
     count = 2 * len(STAGES)
     dma = pltpu.SemaphoreType.DMA
-    return pl.pallas_call(
+    both = pl.pallas_call(
         kernel,
-        out_shape=(out, out),
-        in_specs=[away, away, away, vmem, away, vmem, vmem, vmem],
-        out_specs=(vmem, vmem),
+        out_shape=jax.ShapeDtypeStruct((4, 128, 128), F32),
+        in_specs=[away] * 8,
+        out_specs=vmem,
         scratch_shapes=[
             pltpu.VMEM((2, 1024, 128), BF16),
             pltpu.VMEM((2, 128, 1024), BF16),
             pltpu.VMEM((2, 128, 1024), BF16),
             pltpu.VMEM((OWN, BLOCK), BF16),
+            pltpu.VMEM((2, MODES), I32),
+            pltpu.VMEM((2, MODES, 128), BF16),
+            pltpu.VMEM((2, 128), I32),
+            pltpu.VMEM((2, 128), I32),
             pltpu.VMEM((SIDE, SIDE, 1, 384), F32),
             pltpu.VMEM((128, BLOCK), BF16),
             pltpu.VMEM((128, PLANE * HEAD), BF16),
@@ -549,13 +558,14 @@
             dma((len(PIPES), 2)),
             dma((len(PIPES), 2)),
             dma((len(PIPES), 2)),
-            dma((4,)),
+            dma((8,)),
         ],
         compiler_params=pltpu.CompilerParams(collective_id=0, has_side_effects=True),
         name="schwarz",
     )(
         loads, stiffness, local_inverse, jnp.swapaxes(coarse_basis, 1, 2), coarse_inverse, coarse_index, left, right
     )
+    return both[0:2], both[2:4]
 
 
 def solution(mesh):

time: 88.4 us -> 85.6 us (0.968)
  Pallas kernels: 85.3 us -> 83.1 us
    unnamed x4 -> x0, local copies, waits for them, and re-layouts: 2.26 us -> none
    pallas_call x1, Pallas kernels: 85.3 us -> 83.1 us  [body(): pl.pallas_call(kernel, out_shape=jax.ShapeDtypeStruct((4, 128, 128), F32)...]
    slice x0 -> x1, local copies, waits for them, and re-layouts: none -> 1.69 us  [body(): return (both[0:2], both[2:4])]
where the time goes in v5:
time: 85.6 us; the launch traced here: 85.5 us
  Pallas kernels  83.1 us (97%)
  local copies, waits for them, and re-layouts  1.69 us (2%)
    pallas_call x1, Pallas kernels, body(): pl.pallas_call(kernel, out_shape=jax.ShapeDtypeStruct((4, 128, 128), F32)...  83.1 us

profile of v5, /device:TPU:1, one launch (start us, length us, event | category | flops | bytes accessed | tf_op | source)
XLA Modules:
  0.0 85.5 jit_solution(14712153963559708359)
XLA Ops:
  0.6 83.1 %schwarz.1 = f32[4,128,128]{2,1,0:T(8,128)} custom-call(bf16[2,1024,128]{2,1,0:T(8,128)(2,1)} %loads_in.1, bf16[2,128,1024]{2,1,0:T(8,128)(2,1)} %stiff_in.1, bf16[2,128,1024]{2,1,0:T(8,128)(2,1)} %linv_in.1, bf16[2,48,128]{2,1,0:T(8,128)(2,1)} %bitcast.1, bf16[96,768]{1,0:T(8,128)(2,1)} %cinv_in.1, s32[2,48]{1,0:T(2,128)} %index_in.1, s32[2,128]{1,0:T(2,128)} %left_in.1, ...), custom_call_target="tpu_custom_call" | custom-call | tf_op jit(solution)/shard_map/schwarz/pallas_call | solution.py:510
  83.8 1.7 %fusion = (f32[2,128,128]{2,1,0:T(8,128)}, f32[2,128,128]{2,1,0:T(8,128)}) fusion(f32[4,128,128]{2,1,0:T(8,128)} %schwarz.1), kind=kLoop, calls=%fused_computation | loop fusion | bytes 524288 | tf_op jit(solution)/shard_map/slice | solution.py:568
